TPU v7x, 256 devices: a whole 4x4x8 slice. The times are simulated.
256 devices in a mesh: sa: 4 (over y), row: 4 (over x), col: 16 (over z, core).
Axes of the slice: x: 4, y: 4, z: 8, core: 2. Of those that a mesh axis runs over, the one named last changes fastest.
Arguments:
- states: float32 [2560, 1024], P(None, 'sa')
- pool: float32 [32768, 1024], P(('row', 'col'), 'sa')
- pick: int32 [16384], P(('row', 'col')), may hold values from 0 to 32767, as said below
- tile_table: int32 [8256, 2], P(('row', 'col')), may hold values from 0 to 127, as said below
Outputs:
- normal_tiles: float32 [8256, 128, 128], P(('row', 'col'), 'sa')
Inputs may be any that keep to these rules, and one draw needn't show every extreme that they name: pick[m] lies in pool rows 2 * 256 * (m // 256) to 2 * 256 * (m // 256 + 1) - 1, and the picks of one such group of 256 centres are distinct. `tile_table`: each row (i, j) has i <= j; every such pair of blocks appears in exactly one row; a row stored on the device at index r of row and c of col names one block whose centres lie on a device at row index r and another whose centres lie on a device at col index c.
All inputs are finite; a program needn't handle non-finite values.
Results may differ from a plain program's by a relative error of at most 0.00033.
Values may be sent and summed in bfloat16 or wider, within the bound.
A program may use at most 128 MiB of HBM per device.

v0:
```python
import math

import jax
import jax.numpy as jnp
from jax import lax
from jax.sharding import PartitionSpec as P

F = 1024
M = 16384
MB = 128


def squared_gap(sample_part, centre_part):
    inner_part = jnp.dot(
        sample_part,
        centre_part.T,
        precision=lax.Precision.HIGHEST,
        preferred_element_type=jnp.float32,
    )
    sample_norms = jnp.sum(sample_part * sample_part, axis=1)[:, None]
    centre_norms = jnp.sum(centre_part * centre_part, axis=1)[None, :]
    return sample_norms + centre_norms - 2.0 * inner_part


def shards(states, pool, pick, tile_table):
    sample_count = states.shape[0]
    owner_index = lax.axis_index(("row", "col"))
    centres = jnp.take(pool, pick - owner_index * pool.shape[0], axis=0)
    wide_samples = lax.all_to_all(states, "sa", split_axis=0, concat_axis=1, tiled=True)
    wide_centres = lax.all_gather(centres, "sa", axis=1, tiled=True)
    distance = squared_gap(wide_samples, wide_centres)
    kernel = jnp.exp((2.0 * F - distance) / (4.0 * math.sqrt(F))).astype(jnp.bfloat16)
    kernel_panel = lax.all_gather(kernel, ("row", "col"), axis=1, tiled=True)
    panel_blocks = kernel_panel.reshape(kernel_panel.shape[0], M // MB, MB)
    tile_count = tile_table.shape[0]
    tile_groups = tile_table.reshape(3, tile_count // 3, 2)

    def products(tile_pairs):
        left_blocks = jnp.take(panel_blocks, tile_pairs[:, 0], axis=1)
        right_blocks = jnp.take(panel_blocks, tile_pairs[:, 1], axis=1)
        summed = jnp.einsum(
            "sga,sgb->gab", left_blocks, right_blocks, preferred_element_type=jnp.float32
        )
        return summed / sample_count

    partial_tiles = lax.map(products, tile_groups).reshape(tile_count, MB, MB)
    return lax.psum_scatter(partial_tiles, "sa", scatter_dimension=1, tiled=True)


def solution(mesh):
    placed = (P(None, "sa"), P(("row", "col"), "sa"), P(("row", "col")), P(("row", "col"), None))
    return jax.shard_map(
        shards, mesh=mesh, in_specs=placed, out_specs=P(("row", "col"), "sa", None), check_vma=False
    )
```

profile of v0, /device:TPU:1, one launch (start us, length us, event | category | flops | bytes accessed | tf_op | source)
XLA Modules:
  0.0 391.3 jit_solution(11058333592931336079)
XLA Ops:
  6.5 0.0 copy-start
  6.5 5.1 %all-to-all-start = ((f32[4,640,256]{2,1,0:T(8,128)}), f32[4,640,256]{2,1,0:T(8,128)S(1)}, u32[]{:S(2)}, u32[]{:S(2)}) async-start(f32[4,640,256]{2,1,0:T(8,128)} %bitcast.55), calls=%async_computation | async-start | bytes 5242880 | tf_op jit(solution)/shard_map/all_to_all | solution.py:29
  11.7 0.0 all-gather.3.cloned.1.call-start
  11.7 0.7 compare_and_fusion.2
  12.4 1.0 gather_fusion.2
  13.4 0.0 copy-start.2
  13.4 0.8 broadcast_select_fusion
  14.2 0.0 all-gather.3.cloned.1.call-update
  14.2 0.0 all-gather.5.cloned.1.call-start
  14.3 36.9 %all-gather.3.cloned.1.call-done = f32[256,1024]{1,0:T(8,128)} async-done(((f32[256,256]{1,0:T(8,128)}), f32[256,1024]{1,0:T(8,128)}) %all-gather.3.cloned.1.call-update) | async-done | bytes 1048592 | tf_op jit(solution)/shard_map/all_gather | solution.py:30
  51.2 1.4 multiply_reduce_fusion.1
  52.5 0.0 all-to-all-done
  52.5 2.1 copy.12
  54.7 0.2 multiply_reduce_fusion
  54.9 5.6 %fusion.18 = bf16[640,256]{0,1:T(8,128)(2,1)} fusion(f32[256,1024]{1,0:T(8,128)} %all-gather.3.cloned.1.call-done, f32[640,1024]{0,1:T(8,128)} %bitcast.53, f32[256]{0:T(256)S(1)} %multiply_reduce_fusion.1, f32[640]{0:T(1024)S(1)} %multiply_reduce_fusion), kind=kOutput, calls=%fused_computation.27 | convolution fusion | flops 2014248960 | bytes 4001280 | tf_op jit(solution)/shard_map/dot_general | solution.py:14
  60.6 0.0 all-gather.5.cloned.1.call-update
  60.6 0.0 reduce-scatter.2.cloned.1.call-start
  60.6 0.1 reshape.24
  60.7 112.9 %all-gather.5.cloned.1.call-done = bf16[640,16384]{0,1:T(8,128)(2,1)} async-done(((bf16[640,256]{0,1:T(8,128)(2,1)}), bf16[640,16384]{0,1:T(8,128)(2,1)}) %all-gather.5.cloned.1.call-update) | async-done | bytes 20971536 | tf_op jit(solution)/shard_map/all_gather | solution.py:33
  173.6 28.2 %copy.14 = bf16[640,128,128]{2,0,1:T(8,128)(2,1)} copy(bf16[640,128,128]{0,2,1:T(8,128)(2,1)} %bitcast.52) | data formatting | bytes 41943040 | tf_op jit(solution)/shard_map/while | solution.py:46
  201.8 102.5 %while.10 = (s32[]{:T(128)}, f32[3,43,128,128]{3,2,1,0:T(8,128)}, s32[3,43,2]{1,0,2:T(4,128)S(1)}, bf16[640,128,128]{2,0,1:T(8,128)(2,1)}, s32[]{:T(128)}) while((s32[]{:T(128)}, f32[3,43,128,128]{3,2,1,0:T(8,128)}, s32[3,43,2]{1,0,2:T(4,128)S(1)}, bf16[640,128,128]{2,0,1:T(8,128)(2,1)}, s32[]{:T(128)}) %tuple.32), condition=%wide.region_3.5_spmd, body=%wide.region_2.4_spmd.sunk | while | flops 909527552 | bytes 45099772 | solution.py:46
  201.8 12.5 %gather_fusion = bf16[43,640,128]{2,1,0:T(8,128)(2,1)} fusion(bf16[640,128,128]{2,0,1:T(8,128)(2,1)} %get-tuple-element.109, s32[1024]{0:T(1024)S(1)} %get-tuple-element.92), kind=kCustom, calls=%fused_computation.1.clone.clone.1 | custom fusion | bytes 14090412 | tf_op jit(solution)/shard_map/while/body/eval_jaxpr/jit(_take)/gather | solution.py:40
  214.3 12.4 %gather_fusion.1 = bf16[43,640,128]{2,1,0:T(8,128)(2,1)} fusion(bf16[640,128,128]{2,0,1:T(8,128)(2,1)} %get-tuple-element.109, s32[1024]{0:T(1024)S(1)} %get-tuple-element.94), kind=kCustom, calls=%fused_computation.clone.clone.1 | custom fusion | bytes 14090412 | tf_op jit(solution)/shard_map/while/body/eval_jaxpr/jit(_take)/gather | solution.py:39
  226.7 9.3 %bitcast_dynamic-update-slice_fusion.2 = f32[3,43,128,128]{3,2,1,0:T(8,128)} fusion(f32[3,43,128,128]{3,2,1,0:T(8,128)} %get-tuple-element.102, s32[]{:T(128)} %get-tuple-element.101, bf16[43,640,128]{2,1,0:T(8,128)(2,1)} %gather_fusion, pred[43]{0:T(512)(128)(4,1)S(1)} %get-tuple-element.93, bf16[43,640,128]{2,1,0:T(8,128)(2,1)} %gather_fusion.1, ...), kind=kOutput, calls=%fused_computation.11.clone.1 | convolution fusion | flops 909524992 | bytes 16908886 | tf_op jit(solution)/shard_map/while/body/eval_jaxpr/sga,sgb->gab/dot_general | solution.py:41
  236.0 12.4 %gather_fusion = bf16[43,640,128]{2,1,0:T(8,128)(2,1)} fusion(bf16[640,128,128]{2,0,1:T(8,128)(2,1)} %get-tuple-element.109, s32[1024]{0:T(1024)S(1)} %get-tuple-element.92), kind=kCustom, calls=%fused_computation.1.clone.clone.1 | custom fusion | bytes 14090412 | tf_op jit(solution)/shard_map/while/body/eval_jaxpr/jit(_take)/gather | solution.py:40
  248.4 12.4 %gather_fusion.1 = bf16[43,640,128]{2,1,0:T(8,128)(2,1)} fusion(bf16[640,128,128]{2,0,1:T(8,128)(2,1)} %get-tuple-element.109, s32[1024]{0:T(1024)S(1)} %get-tuple-element.94), kind=kCustom, calls=%fused_computation.clone.clone.1 | custom fusion | bytes 14090412 | tf_op jit(solution)/shard_map/while/body/eval_jaxpr/jit(_take)/gather | solution.py:39
  260.8 9.4 %bitcast_dynamic-update-slice_fusion.2 = f32[3,43,128,128]{3,2,1,0:T(8,128)} fusion(f32[3,43,128,128]{3,2,1,0:T(8,128)} %get-tuple-element.102, s32[]{:T(128)} %get-tuple-element.101, bf16[43,640,128]{2,1,0:T(8,128)(2,1)} %gather_fusion, pred[43]{0:T(512)(128)(4,1)S(1)} %get-tuple-element.93, bf16[43,640,128]{2,1,0:T(8,128)(2,1)} %gather_fusion.1, ...), kind=kOutput, calls=%fused_computation.11.clone.1 | convolution fusion | flops 909524992 | bytes 16908886 | tf_op jit(solution)/shard_map/while/body/eval_jaxpr/sga,sgb->gab/dot_general | solution.py:41
  270.2 12.5 %gather_fusion = bf16[43,640,128]{2,1,0:T(8,128)(2,1)} fusion(bf16[640,128,128]{2,0,1:T(8,128)(2,1)} %get-tuple-element.109, s32[1024]{0:T(1024)S(1)} %get-tuple-element.92), kind=kCustom, calls=%fused_computation.1.clone.clone.1 | custom fusion | bytes 14090412 | tf_op jit(solution)/shard_map/while/body/eval_jaxpr/jit(_take)/gather | solution.py:40
  282.7 12.4 %gather_fusion.1 = bf16[43,640,128]{2,1,0:T(8,128)(2,1)} fusion(bf16[640,128,128]{2,0,1:T(8,128)(2,1)} %get-tuple-element.109, s32[1024]{0:T(1024)S(1)} %get-tuple-element.94), kind=kCustom, calls=%fused_computation.clone.clone.1 | custom fusion | bytes 14090412 | tf_op jit(solution)/shard_map/while/body/eval_jaxpr/jit(_take)/gather | solution.py:39
  295.1 9.3 %bitcast_dynamic-update-slice_fusion.2 = f32[3,43,128,128]{3,2,1,0:T(8,128)} fusion(f32[3,43,128,128]{3,2,1,0:T(8,128)} %get-tuple-element.102, s32[]{:T(128)} %get-tuple-element.101, bf16[43,640,128]{2,1,0:T(8,128)(2,1)} %gather_fusion, pred[43]{0:T(512)(128)(4,1)S(1)} %get-tuple-element.93, bf16[43,640,128]{2,1,0:T(8,128)(2,1)} %gather_fusion.1, ...), kind=kOutput, calls=%fused_computation.11.clone.1 | convolution fusion | flops 909524992 | bytes 16908886 | tf_op jit(solution)/shard_map/while/body/eval_jaxpr/sga,sgb->gab/dot_general | solution.py:41
  304.3 0.0 reduce-scatter.2.cloned.1.call-update
  304.4 80.5 %reduce-scatter.2.cloned.1.call-done = f32[129,32,128]{2,1,0:T(8,128)} async-done(((f32[129,128,128]{2,1,0:T(8,128)}), f32[129,32,128]{2,1,0:T(8,128)}) %reduce-scatter.2.cloned.1.call-update) | async-done | bytes 2113552 | tf_op jit(solution)/shard_map/reduce_scatter | solution.py:47
  (15 shorter events, 0.1 us)
Async XLA Ops:
  6.5 5.8 %copy-start = (f32[512,256]{1,0:T(8,128)S(1)}, f32[512,256]{1,0:T(8,128)}, u32[]{:S(2)}) copy-start(f32[512,256]{1,0:T(8,128)} %param.9) | copy-start | bytes 1572868
  6.5 46.0 %all-to-all-start = ((f32[4,640,256]{2,1,0:T(8,128)}), f32[4,640,256]{2,1,0:T(8,128)S(1)}, u32[]{:S(2)}, u32[]{:S(2)}) async-start(f32[4,640,256]{2,1,0:T(8,128)} %bitcast.55), calls=%async_computation | async-start | bytes 5242880 | tf_op jit(solution)/shard_map/all_to_all | solution.py:29
  11.7 39.5 %all-gather.3.cloned.1.call-start = ((), (), s32[]{:S(2)}) async-start(), calls=%async_computation.2 | async-start | bytes 1310720 | tf_op jit(solution)/shard_map/all_gather | solution.py:30
  13.4 47.3 %copy-start.2 = (s32[129,2]{0,1:T(2,128)S(1)}, s32[129,2]{0,1:T(2,128)}, u32[]{:S(2)}) copy-start(s32[129,2]{0,1:T(2,128)} %param.11) | copy-start | bytes 3100
  14.2 159.4 %all-gather.5.cloned.1.call-start = ((), (), s32[]{:S(2)}) async-start(), calls=%async_computation.3 | async-start | bytes 21299200 | tf_op jit(solution)/shard_map/all_gather | solution.py:33
  60.6 324.2 %reduce-scatter.2.cloned.1.call-start = ((), (), s32[]{:S(2)}) async-start(), calls=%async_computation.4 | async-start | bytes 10567680 | tf_op jit(solution)/shard_map/reduce_scatter | solution.py:47
  304.3 80.5 %copy-start.1 = (f32[512,256]{1,0:T(8,128)S(1)}, f32[512,256]{1,0:T(8,128)}, u32[]{:S(2)}) copy-start(f32[512,256]{1,0:T(8,128)} %param.9) | copy-start | bytes 1572868
Sparse Core Ops, SparseCore 0:
  14.3 36.7 all-gather.2
  60.7 112.8 all-gather.4
  304.5 80.2 reduce-scatter.1
where the time goes:
time: 392 us; the launch traced here: 391 us
  waiting for transfers between devices  230 us (59%)
  local copies, waits for them, and re-layouts  106 us (27%)
  matrix products  33.6 us (9%)
  between operations  13.2 us (3%)
  starting transfers between devices  5.23 us (1%)
    all_gather x1, waiting for transfers between devices, shards(): kernel_panel = lax.all_gather(kernel, ('row', 'col'), axis=1, tiled=True)  113 us
    reduce_scatter x1, waiting for transfers between devices, shards(): lax.psum_scatter(partial_tiles, 'sa', scatter_dimension=1, tiled=True)  80.5 us
    gather x3, local copies, waits for them, and re-layouts, products(): right_blocks = jnp.take(panel_blocks, tile_pairs[:, 1], axis=1)  37.3 us
    gather x3, local copies, waits for them, and re-layouts, products(): left_blocks = jnp.take(panel_blocks, tile_pairs[:, 0], axis=1)  37.2 us
    all_gather x1, waiting for transfers between devices, shards(): wide_centres = lax.all_gather(centres, 'sa', axis=1, tiled=True)  36.9 us
    while x1, local copies, waits for them, and re-layouts, shards(): partial_tiles = lax.map(products, tile_groups).reshape(tile_count, MB, MB)  28.2 us
    dot_general x3, matrix products, products(): jnp.einsum('sga,sgb->gab', left_blocks, right_blocks, preferred_element_t...  28 us
  transfers between devices with their start and end apart: 4, of which 3 were waited for; matrix products, arithmetic and copies ran while one was open for 1% of the time, Pallas kernels for 0%

commit v1 on v0

v1 whole, which is shorter than its diff:
```python
import functools
import math

import jax
import jax.numpy as jnp
from jax import lax
from jax.experimental import pallas as pl
from jax.experimental.pallas import tpu as pltpu
from jax.sharding import PartitionSpec as P

F = 1024
M = 16384
MB = 128
N_SA = 4
N_ROW = 4
N_COL = 16
QUART = MB // N_SA


def products_kernel(where_ref, table_ref, r_ref, c_ref, o_ref, g1, g2, rq, cq, *, samples):
    step = pl.program_id(0)
    quarter, row, col = where_ref[0], where_ref[1], where_ref[2]
    nt = (((1,), (1,)), ((), ()))

    @pl.when(step == 0)
    def _():
        g1[...] = jnp.zeros_like(g1)
        g2[...] = jnp.zeros_like(g2)

    def rows(half):
        return pl.ds(pl.multiple_of(half * MB + quarter * QUART, QUART), QUART)

    for dev in range(N_COL):
        for half in range(2):
            rq[(dev * 2 + half) * QUART:(dev * 2 + half + 1) * QUART, :] = r_ref[0, dev, rows(half), :]
    for dev in range(N_ROW):
        for half in range(2):
            cq[(dev * 2 + half) * QUART:(dev * 2 + half + 1) * QUART, :] = c_ref[0, dev, rows(half), :]

    @pl.loop(0, 4)
    def _(m):
        top = pl.ds(pl.multiple_of(m * 256, 256), 256)
        for dev in range(N_ROW):
            got = lax.dot_general(rq[top, :], c_ref[0, dev], nt, preferred_element_type=jnp.float32)
            for half in range(2):
                g1[dev * 2 + half, top, :] += got[:, half * MB:(half + 1) * MB]

    @pl.loop(0, N_COL)
    def _(dev):
        got = lax.dot_general(cq[...], r_ref[0, dev], nt, preferred_element_type=jnp.float32)
        for half in range(2):
            g2[dev * 2 + half, :, :] += got[:, half * MB:(half + 1) * MB]

    @pl.when(step == pl.num_programs(0) - 1)
    def _():
        @pl.loop(0, o_ref.shape[0])
        def _(k):
            i, j = table_ref[0, k], table_ref[1, k]
            row_i, col_i, half_i = i // (2 * N_COL), (i // 2) % N_COL, i % 2
            row_j, col_j, half_j = j // (2 * N_COL), (j // 2) % N_COL, j % 2
            straight = jnp.logical_and(row_i == row, col_j == col)

            @pl.when(straight)
            def _():
                top = pl.ds(pl.multiple_of((col_i * 2 + half_i) * QUART, QUART), QUART)
                o_ref[k] = g1[row_j * 2 + half_j, top, :] / samples

            @pl.when(jnp.logical_not(straight))
            def _():
                top = pl.ds(pl.multiple_of((row_i * 2 + half_i) * QUART, QUART), QUART)
                o_ref[k] = g2[col_j * 2 + half_j, top, :] / samples


def tile_products(where, table, r_all, c_all):
    steps, _, cent, count = r_all.shape
    tiles = table.shape[1]
    return pl.pallas_call(
        functools.partial(products_kernel, samples=float(steps * count)),
        out_shape=jax.ShapeDtypeStruct((tiles, QUART, MB), jnp.float32),
        grid_spec=pltpu.PrefetchScalarGridSpec(
            num_scalar_prefetch=2,
            grid=(steps,),
            in_specs=[
                pl.BlockSpec((1, N_COL, cent, count), lambda q, *_: (q, 0, 0, 0)),
                pl.BlockSpec((1, N_ROW, cent, count), lambda q, *_: (q, 0, 0, 0)),
            ],
            out_specs=pl.BlockSpec((tiles, QUART, MB), lambda q, *_: (0, 0, 0)),
            scratch_shapes=[
                pltpu.VMEM((2 * N_ROW, 2 * N_COL * QUART, MB), jnp.float32),
                pltpu.VMEM((2 * N_COL, 2 * N_ROW * QUART, MB), jnp.float32),
                pltpu.VMEM((2 * N_COL * QUART, count), jnp.bfloat16),
                pltpu.VMEM((2 * N_ROW * QUART, count), jnp.bfloat16),
            ],
        ),
        compiler_params=pltpu.CompilerParams(
            dimension_semantics=("arbitrary",), vmem_limit_bytes=48 * 2**20
        ),
    )(where, table, r_all, c_all)


def partial_distance(states, centres):
    parts = states.reshape(N_SA, states.shape[0] // N_SA, states.shape[1])
    inner = jnp.einsum(
        "cf,qsf->qcs", centres, parts, precision=lax.Precision.HIGHEST, preferred_element_type=jnp.float32
    )
    sample_norms = jnp.sum(parts * parts, axis=2)[:, None, :]
    centre_norms = jnp.sum(centres * centres, axis=1)[None, :, None]
    return sample_norms + centre_norms - 2.0 * inner


def shards(states, pool, pick, tile_table):
    quarter, row, col = lax.axis_index("sa"), lax.axis_index("row"), lax.axis_index("col")
    local = pick - (row * N_COL + col) * pool.shape[0]
    centres = pool.at[local].get(mode="promise_in_bounds")
    distance = lax.psum_scatter(partial_distance(states, centres), "sa", scatter_dimension=0, tiled=False)
    kernel = jnp.exp((2.0 * F - distance) / (4.0 * math.sqrt(F))).astype(jnp.bfloat16)
    cent, count = kernel.shape
    r_all = lax.all_gather(kernel, ("sa", "col")).reshape(N_SA, N_COL, cent, count)
    c_all = lax.all_gather(kernel, ("sa", "row")).reshape(N_SA, N_ROW, cent, count)
    where = jnp.stack([quarter, row, col]).astype(jnp.int32)
    return tile_products(where, tile_table.T, r_all, c_all)


def solution(mesh):
    placed = (P(None, "sa"), P(("row", "col"), "sa"), P(("row", "col")), P(("row", "col"), None))
    return jax.shard_map(
        shards, mesh=mesh, in_specs=placed, out_specs=P(("row", "col"), "sa", None), check_vma=False
    )
```

time: 392 us -> 282 us (0.72)
  local copies, waits for them, and re-layouts: 106 us -> 3.48 us
  Pallas kernels: 0 us -> 40.2 us
  matrix products: 33.6 us -> 4.02 us
  waiting for transfers between devices: 230 us -> 216 us
  starting transfers between devices: 5.23 us -> 0.09 us
    gather x7 -> x1, local copies, waits for them, and re-layouts: 75.5 us -> 0.97 us  [shards(): centres = pool.at[local].get(mode='promise_in_bounds')]
    pallas_call x0 -> x1, Pallas kernels: none -> 40.2 us  [tile_products(): pl.pallas_call(functools.partial(products_kernel, samples=float(steps * c...]
    reduce_scatter x1, waiting for transfers between devices: 80.5 us -> 40.5 us  [shards(): lax.psum_scatter(partial_distance(states, centres), 'sa', scatter_dimensi...]
    dot_general x4 -> x1, matrix products: 33.6 us -> 4.02 us  [partial_distance(): jnp.einsum('cf,qsf->qcs', centres, parts, precision=lax.Precision.HIGHEST...]
    while x1 -> x0, local copies, waits for them, and re-layouts: 28.2 us -> none  [shards(): partial_tiles = lax.map(products, tile_groups).reshape(tile_count, MB, MB)]
    all_gather x2, waiting for transfers between devices: 150 us -> 174 us  [the longest x1 114 us: shards(): lax.all_gather(kernel, ('sa', 'col')).reshape(N_SA, N_COL, cent, count)]
    all_to_all x1 -> x0, starting transfers between devices: 5.14 us -> none  [shards(): lax.all_to_all(states, 'sa', split_axis=0, concat_axis=1, tiled=True)]
  transfers between devices with their start and end apart: 4 -> 3, of which waited for: 3 -> 3; matrix products, arithmetic and copies ran while one was open for 1% -> 0% of each run, Pallas kernels for 0% -> 0%
where the time goes in v1:
time: 282 us
  waiting for transfers between devices  216 us (77%)
  Pallas kernels  40.2 us (14%)
  between operations  13.2 us (5%)
  other arithmetic  5.15 us (2%)
  matrix products  4.02 us (1%)
  local copies, waits for them, and re-layouts  3.48 us (1%)
    all_gather x1, waiting for transfers between devices, shards(): lax.all_gather(kernel, ('sa', 'col')).reshape(N_SA, N_COL, cent, count)  114 us
    all_gather x1, waiting for transfers between devices, shards(): lax.all_gather(kernel, ('sa', 'row')).reshape(N_SA, N_ROW, cent, count)  60.8 us
    reduce_scatter x1, waiting for transfers between devices, shards(): lax.psum_scatter(partial_distance(states, centres), 'sa', scatter_dimensi...  40.5 us
    pallas_call x1, Pallas kernels, tile_products(): pl.pallas_call(functools.partial(products_kernel, samples=float(steps * c...  40.2 us
  transfers between devices with their start and end apart: 3, of which 3 were waited for; matrix products, arithmetic and copies ran while one was open for 0% of the time, Pallas kernels for 0%

profile of v1, /device:TPU:1, one launch (start us, length us, event | category | flops | bytes accessed | tf_op | source)
XLA Modules:
  0.0 281.7 jit_solution(8785088194985527495)
XLA Ops:
  6.5 0.0 copy-start
  6.5 0.0 reduce-scatter.2.cloned.1.call-start
  6.5 0.7 compare_select_fusion
  7.3 0.0 copy-start.3
  7.3 2.3 multiply_reduce_fusion
  9.6 0.0 copy-done
  9.6 1.0 gather_fusion
  10.6 0.1 multiply_reduce_fusion.1
  10.7 0.0 copy-done.3
  10.7 4.0 %bitcast_subtract_fusion = f32[4,256,640]{2,1,0:T(8,128)} fusion(f32[4,640,256]{2,1,0:T(8,128)S(1)} %bitcast.16, f32[256]{0:T(256)S(1)} %multiply_reduce_fusion.1, f32[4,640]{1,0:T(4,128)S(1)} %add.26, f32[256,256]{1,0:T(8,128)S(1)} %gather_fusion), kind=kOutput, calls=%fused_computation.1 | convolution fusion | flops 2015232000 | bytes 5516288 | tf_op jit(solution)/shard_map/cf,qsf->qcs/dot_general | solution.py:103
  14.7 0.0 copy-start.2
  14.7 0.0 reduce-scatter.2.cloned.1.call-update
  14.8 0.0 all-gather.5.cloned.1.call-start
  14.8 40.5 %reduce-scatter.2.cloned.1.call-done = f32[1,256,640]{2,1,0:T(8,128)} async-done(((f32[4,256,640]{2,1,0:T(8,128)}), f32[1,256,640]{2,1,0:T(8,128)}) %reduce-scatter.2.cloned.1.call-update) | async-done | bytes 655376 | tf_op jit(solution)/shard_map/reduce_scatter | solution.py:115
  55.3 1.9 exponential_convert_fusion
  57.2 0.0 all-gather.5.cloned.1.call-update
  57.3 0.0 all-gather.3.cloned.1.call-start
  57.3 0.7 all-gather.3.cloned.1.call-update
  58.0 0.1 pad_add_fusion.where_ref
  58.1 60.8 %all-gather.5.cloned.1.call-done = bf16[16,256,640]{2,1,0:T(8,128)(2,1)} async-done(((bf16[1,256,640]{2,1,0:T(8,128)(2,1)}), bf16[16,256,640]{2,1,0:T(8,128)(2,1)}) %all-gather.5.cloned.1.call-update) | async-done | bytes 5242896 | tf_op jit(solution)/shard_map/all_gather | solution.py:119
  118.9 113.6 %all-gather.3.cloned.1.call-done = bf16[64,256,640]{2,1,0:T(8,128)(2,1)} async-done(((bf16[1,256,640]{2,1,0:T(8,128)(2,1)}), bf16[64,256,640]{2,1,0:T(8,128)(2,1)}) %all-gather.3.cloned.1.call-update) | async-done | bytes 20971536 | tf_op jit(solution)/shard_map/all_gather | solution.py:118
  232.4 0.0 copy-done.2
  232.4 0.0 copy-start.1
  232.4 2.5 copy-done.1
  234.9 40.2 %shard_map.46 = f32[129,32,128]{2,1,0:T(8,128)} custom-call(s32[3]{0:T(128)S(1)} %pad_add_fusion.where_ref, s32[2,129]{1,0:T(2,128)S(1)} %bitcast.14, bf16[4,16,256,640]{3,2,1,0:T(8,128)(2,1)} %bitcast.15, bf16[4,4,256,640]{3,2,1,0:T(8,128)(2,1)S(1)} %bitcast.13), custom_call_target="tpu_custom_call" | custom-call | tf_op jit(solution)/shard_map/pallas_call | solution.py:77
  (2 shorter events, 0.0 us)
Async XLA Ops:
  6.5 3.1 %copy-start = (f32[512,256]{1,0:T(8,128)S(1)}, f32[512,256]{1,0:T(8,128)}, u32[]{:S(2)}) copy-start(f32[512,256]{1,0:T(8,128)} %param.5) | copy-start | bytes 1572868
  6.5 48.8 %reduce-scatter.2.cloned.1.call-start = ((), (), s32[]{:S(2)}) async-start(), calls=%async_computation.1 | async-start | bytes 3276800 | tf_op jit(solution)/shard_map/reduce_scatter | solution.py:115
  7.3 3.4 %copy-start.3 = (f32[2560,256]{1,0:T(8,128)S(1)}, f32[2560,256]{1,0:T(8,128)}, u32[]{:S(2)}) copy-start(f32[2560,256]{1,0:T(8,128)} %param.4) | copy-start | bytes 7864324
  14.7 217.7 %copy-start.2 = (s32[129,2]{0,1:T(2,128)S(1)}, s32[129,2]{0,1:T(2,128)}, u32[]{:S(2)}) copy-start(s32[129,2]{0,1:T(2,128)} %param.7) | copy-start | bytes 3100
  14.8 104.1 %all-gather.5.cloned.1.call-start = ((), (), s32[]{:S(2)}) async-start(), calls=%async_computation.3 | async-start | bytes 5570560 | tf_op jit(solution)/shard_map/all_gather | solution.py:119
  57.3 175.2 %all-gather.3.cloned.1.call-start = ((), (), s32[]{:S(2)}) async-start(), calls=%async_computation.2 | async-start | bytes 21299200 | tf_op jit(solution)/shard_map/all_gather | solution.py:118
  232.4 2.5 copy-start.1
Sparse Core Ops, SparseCore 0:
  14.9 40.3 reduce-scatter.1
  57.8 61.0 all-gather.4
  121.6 110.7 all-gather.2

commit v2 on v1

--- a/solution.py
+++ b/solution.py
@@ -1,4 +1,5 @@
 import functools
+import heapq
 import math
 
 import jax
@@ -14,7 +15,195 @@
 N_SA = 4
 N_ROW = 4
 N_COL = 16
+N_Z = 8
 QUART = MB // N_SA
+CENT = 256
+COUNT = 640
+SPLIT = 384
+ALL_ROWS = (0, CENT)
+LOW_ROWS = (0, CENT // 2)
+HIGH_ROWS = (CENT // 2, CENT)
+ALL_COLS = (0, COUNT)
+Z_FIRST = (0, SPLIT)
+Y_FIRST = (SPLIT, COUNT)
+
+
+class Send:
+    def __init__(self, link, src, dst, rows, cols, deps, rank):
+        self.link, self.src, self.dst, self.rows, self.cols = link, src, dst, rows, cols
+        self.deps, self.rank = deps, rank
+
+    def size(self):
+        return 2 * (self.rows[1] - self.rows[0]) * (self.cols[1] - self.cols[0])
+
+
+def spread_plan():
+    sends = []
+
+    def add(*args):
+        sends.append(Send(*args))
+        return len(sends) - 1
+
+    def ring(axis, size, slot_of, start, cols, deps, rank):
+        filled = {}
+        for sign, half in (("+", LOW_ROWS), ("-", HIGH_ROWS)):
+            step = -1 if sign == "+" else 1
+            need, at = deps, start
+            for hop in range(1, size // 2 + 1):
+                rows = half if hop == size // 2 else ALL_ROWS
+                to = (at + step) % size
+                k = add(axis + sign, slot_of(at), slot_of(to), rows, cols, need, rank + hop)
+                filled.setdefault(to, []).append(k)
+                need, at = [k], to
+        return filled
+
+    y_own = ring("y", N_SA, lambda d: ("R", d, 0, 0), 0, ALL_COLS, [], 0)
+    z_own = ring("z", N_Z, lambda d: ("R", 0, d, 0), 0, Z_FIRST, [], 0)
+    arrived = {}
+    for dz in range(1, N_Z):
+        arrived[0, dz, Z_FIRST] = z_own[dz]
+        got = ring("y", N_SA, lambda d: ("R", d, dz, 0), 0, Z_FIRST, z_own[dz], 10)
+        for dy in range(1, N_SA):
+            arrived[dy, dz, Z_FIRST] = got[dy]
+    for dy in range(N_SA):
+        need = y_own[dy] if dy else []
+        got = ring("z", N_Z, lambda d: ("R", dy, d, 0), 0, Y_FIRST, need, 10)
+        for dz in range(1, N_Z):
+            arrived[dy, dz, Y_FIRST] = got[dz]
+        ring("x", N_ROW, lambda d: ("C", dy, d) if d else ("R", dy, 0, 0), 0, ALL_COLS, need, 20)
+        add("s", ("R", dy, 0, 0), ("R", dy, 0, 1), ALL_ROWS, ALL_COLS, need, 30)
+    for (dy, dz, cols), need in arrived.items():
+        add("s", ("R", dy, dz, 0), ("R", dy, dz, 1), ALL_ROWS, cols, need, 30)
+    return sends
+
+
+def spread_order(sends):
+    rate = {"s": 200e3}
+    free, pending, done, events, queue = {}, set(range(len(sends))), set(), [], []
+
+    def start_ready(now):
+        ready = sorted((k for k in pending if all(d in done for d in sends[k].deps)), key=lambda k: (sends[k].rank, k))
+        for k in ready:
+            pending.discard(k)
+            link = sends[k].link
+            begin = max(now, free.get(link, 0.0))
+            free[link] = begin + sends[k].size() / rate.get(link, 46e3)
+            heapq.heappush(queue, (free[link] + 1.7, k))
+        return ready
+
+    events.append((None, start_ready(0.0)))
+    while queue:
+        now, k = heapq.heappop(queue)
+        done.add(k)
+        events.append((k, start_ready(now)))
+    return events, max(free.values())
+
+
+def spread_kernel(sends, events, part, r_out, c_out, from_low, from_high, merge, kernel_own, rs_send, rs_recv, out_sems,
+                  in_sems, own_sem):
+    y, x, col = lax.axis_index("sa"), lax.axis_index("row"), lax.axis_index("col")
+    z, core = col // 2, col % 2
+    yp, yo, ym = (y + 1) % N_SA, (y + 2) % N_SA, (y + 3) % N_SA
+    to = {
+        "y+": {"sa": yp},
+        "y-": {"sa": ym},
+        "x+": {"row": (x + 1) % N_ROW},
+        "x-": {"row": (x + 3) % N_ROW},
+        "z+": {"col": (z + 1) % N_Z * 2 + core},
+        "z-": {"col": (z + 7) % N_Z * 2 + core},
+        "s": {"col": z * 2 + 1 - core},
+    }
+    mesh_id = pl.DeviceIdType.MESH
+    barrier = pltpu.get_barrier_semaphore()
+    for peer in to.values():
+        pl.semaphore_signal(barrier, inc=1, device_id=peer, device_id_type=mesh_id)
+    pl.semaphore_wait(barrier, len(to))
+
+    low, high = pl.ds(0, CENT // 2), pl.ds(CENT // 2, CENT // 2)
+
+    def rs(src, buf, slot, link):
+        way = 0 if link == "y+" else 3
+        copy = pltpu.make_async_remote_copy(
+            src_ref=src, dst_ref=buf.at[slot], send_sem=rs_send.at[way + slot], recv_sem=rs_recv.at[way + slot],
+            device_id=to[link], device_id_type=mesh_id)
+        copy.start()
+        return copy
+
+    copies = [
+        rs(part.at[yo, low], from_low, 0, "y+"),
+        rs(part.at[yo, high], from_high, 0, "y-"),
+        rs(part.at[yp, high], from_low, 1, "y+"),
+        rs(part.at[ym, low], from_high, 1, "y-"),
+    ]
+    copies[0].wait_recv()
+    merge[0] = part[yp, :CENT // 2] + from_low[0]
+    copies.append(rs(merge.at[0], from_low, 2, "y+"))
+    copies[1].wait_recv()
+    merge[1] = part[ym, CENT // 2:] + from_high[0]
+    copies.append(rs(merge.at[1], from_high, 2, "y-"))
+    for k in range(2, 6):
+        copies[k].wait_recv()
+    low_sum = part[y, :CENT // 2] + from_low[2] + from_high[1]
+    kernel_own[:CENT // 2] = jnp.exp((2.0 * F - low_sum) / (4.0 * math.sqrt(F))).astype(jnp.bfloat16)
+    high_sum = part[y, CENT // 2:] + from_low[1] + from_high[2]
+    kernel_own[CENT // 2:] = jnp.exp((2.0 * F - high_sum) / (4.0 * math.sqrt(F))).astype(jnp.bfloat16)
+    for copy in copies:
+        copy.wait_send()
+
+    own = pltpu.make_async_copy(kernel_own, r_out.at[0, 0], own_sem)
+    own.start()
+
+    def slot(place, rows, cols, source):
+        rows, cols = pl.ds(rows[0], rows[1] - rows[0]), pl.ds(cols[0], cols[1] - cols[0])
+        if source and place == ("R", 0, 0, 0):
+            return kernel_own.at[rows, cols]
+        if place[0] == "R":
+            return r_out.at[place[1], place[2] * 2 + place[3], rows, cols]
+        return c_out.at[place[1], place[2] - 1, rows, cols]
+
+    started = {}
+    for k, send in enumerate(sends):
+        started[k] = pltpu.make_async_remote_copy(
+            src_ref=slot(send.src, send.rows, send.cols, True), dst_ref=slot(send.dst, send.rows, send.cols, False),
+            send_sem=out_sems.at[k], recv_sem=in_sems.at[k], device_id=to[send.link], device_id_type=mesh_id)
+    for arrival, ready in events:
+        if arrival is not None:
+            started[arrival].wait_recv()
+        for k in ready:
+            started[k].start()
+    own.wait()
+    for copy in started.values():
+        copy.wait_send()
+
+
+def spread(part):
+    sends = spread_plan()
+    events, _ = spread_order(sends)
+    half = (CENT // 2, COUNT)
+    anywhere = pl.BlockSpec(memory_space=pl.ANY)
+    return pl.pallas_call(
+        functools.partial(spread_kernel, sends, events),
+        out_shape=(
+            jax.ShapeDtypeStruct((N_SA, N_COL, CENT, COUNT), jnp.bfloat16),
+            jax.ShapeDtypeStruct((N_SA, N_ROW - 1, CENT, COUNT), jnp.bfloat16),
+        ),
+        in_specs=[pl.BlockSpec(memory_space=pltpu.VMEM)],
+        out_specs=(anywhere, anywhere),
+        scratch_shapes=[
+            pltpu.VMEM((3, *half), jnp.float32),
+            pltpu.VMEM((3, *half), jnp.float32),
+            pltpu.VMEM((2, *half), jnp.float32),
+            pltpu.VMEM((CENT, COUNT), jnp.bfloat16),
+            pltpu.SemaphoreType.DMA((6,)),
+            pltpu.SemaphoreType.DMA((6,)),
+            pltpu.SemaphoreType.DMA((len(sends),)),
+            pltpu.SemaphoreType.DMA((len(sends),)),
+            pltpu.SemaphoreType.DMA,
+        ],
+        compiler_params=pltpu.CompilerParams(
+            collective_id=0, has_side_effects=True, vmem_limit_bytes=24 * 2**20
+        ),
+    )(part)
 
 
 def products_kernel(where_ref, table_ref, r_ref, c_ref, o_ref, g1, g2, rq, cq, *, samples):
@@ -29,19 +218,22 @@
 
     def rows(half):
         return pl.ds(pl.multiple_of(half * MB + quarter * QUART, QUART), QUART)
+
+    def column(dev):
+        return c_ref.at[0, dev - 1] if dev else r_ref.at[0, 0]
 
     for dev in range(N_COL):
         for half in range(2):
             rq[(dev * 2 + half) * QUART:(dev * 2 + half + 1) * QUART, :] = r_ref[0, dev, rows(half), :]
     for dev in range(N_ROW):
         for half in range(2):
-            cq[(dev * 2 + half) * QUART:(dev * 2 + half + 1) * QUART, :] = c_ref[0, dev, rows(half), :]
+            cq[(dev * 2 + half) * QUART:(dev * 2 + half + 1) * QUART, :] = column(dev)[rows(half), :]
 
     @pl.loop(0, 4)
     def _(m):
         top = pl.ds(pl.multiple_of(m * 256, 256), 256)
         for dev in range(N_ROW):
-            got = lax.dot_general(rq[top, :], c_ref[0, dev], nt, preferred_element_type=jnp.float32)
+            got = lax.dot_general(rq[top, :], column(dev)[...], nt, preferred_element_type=jnp.float32)
             for half in range(2):
                 g1[dev * 2 + half, top, :] += got[:, half * MB:(half + 1) * MB]
 
@@ -60,15 +252,21 @@
             row_j, col_j, half_j = j // (2 * N_COL), (j // 2) % N_COL, j % 2
             straight = jnp.logical_and(row_i == row, col_j == col)
 
+            def far_col(c):
+                return (c // 2 - col // 2 + N_Z) % N_Z * 2 + (c + col) % 2
+
+            def far_row(r):
+                return (r - row + N_ROW) % N_ROW
+
             @pl.when(straight)
             def _():
-                top = pl.ds(pl.multiple_of((col_i * 2 + half_i) * QUART, QUART), QUART)
-                o_ref[k] = g1[row_j * 2 + half_j, top, :] / samples
+                top = pl.ds(pl.multiple_of((far_col(col_i) * 2 + half_i) * QUART, QUART), QUART)
+                o_ref[k] = g1[far_row(row_j) * 2 + half_j, top, :] / samples
 
             @pl.when(jnp.logical_not(straight))
             def _():
-                top = pl.ds(pl.multiple_of((row_i * 2 + half_i) * QUART, QUART), QUART)
-                o_ref[k] = g2[col_j * 2 + half_j, top, :] / samples
+                top = pl.ds(pl.multiple_of((far_row(row_i) * 2 + half_i) * QUART, QUART), QUART)
+                o_ref[k] = g2[far_col(col_j) * 2 + half_j, top, :] / samples
 
 
 def tile_products(where, table, r_all, c_all):
@@ -82,7 +280,7 @@
             grid=(steps,),
             in_specs=[
                 pl.BlockSpec((1, N_COL, cent, count), lambda q, *_: (q, 0, 0, 0)),
-                pl.BlockSpec((1, N_ROW, cent, count), lambda q, *_: (q, 0, 0, 0)),
+                pl.BlockSpec((1, N_ROW - 1, cent, count), lambda q, *_: (q, 0, 0, 0)),
             ],
             out_specs=pl.BlockSpec((tiles, QUART, MB), lambda q, *_: (0, 0, 0)),
             scratch_shapes=[
@@ -112,11 +310,7 @@
     quarter, row, col = lax.axis_index("sa"), lax.axis_index("row"), lax.axis_index("col")
     local = pick - (row * N_COL + col) * pool.shape[0]
     centres = pool.at[local].get(mode="promise_in_bounds")
-    distance = lax.psum_scatter(partial_distance(states, centres), "sa", scatter_dimension=0, tiled=False)
-    kernel = jnp.exp((2.0 * F - distance) / (4.0 * math.sqrt(F))).astype(jnp.bfloat16)
-    cent, count = kernel.shape
-    r_all = lax.all_gather(kernel, ("sa", "col")).reshape(N_SA, N_COL, cent, count)
-    c_all = lax.all_gather(kernel, ("sa", "row")).reshape(N_SA, N_ROW, cent, count)
+    r_all, c_all = spread(partial_distance(states, centres))
     where = jnp.stack([quarter, row, col]).astype(jnp.int32)
     return tile_products(where, tile_table.T, r_all, c_all)
 

time: 282 us -> 151 us (0.54)
  waiting for transfers between devices: 216 us -> 0 us
  Pallas kernels: 40.2 us -> 137 us
  between operations: 13.2 us -> 0.07 us
  local copies, waits for them, and re-layouts: 3.48 us -> 7.96 us
    all_gather x2 -> x0, waiting for transfers between devices: 174 us -> none  [the longest x1 114 us: shards(): lax.all_gather(kernel, ('sa', 'col')).reshape(N_SA, N_COL, cent, count)]
    pallas_call x0 -> x1, Pallas kernels: none -> 94.2 us  [spread(): pl.pallas_call(functools.partial(spread_kernel, sends, events), out_shape...]
    reduce_scatter x1 -> x0, waiting for transfers between devices: 40.5 us -> none  [shards(): lax.psum_scatter(partial_distance(states, centres), 'sa', scatter_dimensi...]
    unnamed x8, local copies, waits for them, and re-layouts: 2.5 us -> 6.98 us
  transfers between devices with their start and end apart: 3 -> 0, of which waited for: 3 -> 0; matrix products, arithmetic and copies ran while one was open for 0% -> 0% of each run, Pallas kernels for 0% -> 0%
where the time goes in v2:
time: 151 us
  Pallas kernels  137 us (91%)
  local copies, waits for them, and re-layouts  7.96 us (5%)
  other arithmetic  3.23 us (2%)
  matrix products  2.52 us (2%)
    pallas_call x1, Pallas kernels, spread(): pl.pallas_call(functools.partial(spread_kernel, sends, events), out_shape...  94.2 us
    pallas_call x1, Pallas kernels, tile_products(): pl.pallas_call(functools.partial(products_kernel, samples=float(steps * c...  42.8 us
    unnamed x8, local copies, waits for them, and re-layouts  6.98 us

profile of v2, /device:TPU:1, one launch (start us, length us, event | category | flops | bytes accessed | tf_op | source)
XLA Modules:
  0.0 150.8 jit_solution(10773728902241154383)
XLA Ops:
  0.0 0.0 copy-start
  0.0 0.1 pad_add_fusion.where_ref
  0.1 0.7 compare_select_fusion
  0.8 0.0 copy-start.3
  0.8 2.3 %multiply_reduce_fusion = f32[2560]{0:T(1024)S(1)} fusion(f32[2560,256]{1,0:T(8,128)} %param.4), kind=kLoop, calls=%fused_computation.2 | loop fusion | flops 1308160 | bytes 2631680 | tf_op jit(solution)/shard_map/reduce_sum | solution.py:304
  3.1 0.0 copy-done
  3.2 1.0 gather_fusion
  4.1 0.1 multiply_reduce_fusion.1
  4.2 0.0 copy-done.3
  4.3 2.5 %bitcast_subtract_fusion.part = f32[4,256,640]{2,1,0:T(8,128)S(1)} fusion(f32[4,640,256]{2,1,0:T(8,128)S(1)} %bitcast.12, f32[256]{0:T(256)S(1)} %multiply_reduce_fusion.1, f32[4,640]{1,0:T(4,128)S(1)} %add.24, f32[256,256]{1,0:T(8,128)S(1)} %gather_fusion), kind=kOutput, calls=%fused_computation.1 | convolution fusion | flops 2015232000 | bytes 5516288 | tf_op jit(solution)/shard_map/cf,qsf->qcs/dot_general | solution.py:301
  6.8 0.0 copy-start.2
  6.8 94.2 %shard_map.46 = (bf16[4,16,256,640]{3,2,1,0:T(8,128)(2,1)S(1)}, bf16[4,3,256,640]{3,2,1,0:T(8,128)(2,1)S(1)}) custom-call(f32[4,256,640]{2,1,0:T(8,128)S(1)} %bitcast_subtract_fusion.part), custom_call_target="tpu_custom_call" | custom-call | tf_op jit(solution)/shard_map/pallas_call | solution.py:184
  101.0 0.0 copy-start.1
  101.0 7.0 %copy-done.1 = bf16[4,16,256,640]{3,2,1,0:T(8,128)(2,1)} copy-done((bf16[4,16,256,640]{3,2,1,0:T(8,128)(2,1)}, bf16[4,16,256,640]{3,2,1,0:T(8,128)(2,1)S(1)}, u32[]{:S(2)}) %copy-start.1) | copy-done | bytes 20971544
  108.0 0.0 copy-done.2
  108.0 42.8 %shard_map.47 = f32[129,32,128]{2,1,0:T(8,128)} custom-call(s32[3]{0:T(128)S(1)} %pad_add_fusion.where_ref, s32[2,129]{1,0:T(2,128)S(1)} %bitcast.11, bf16[4,16,256,640]{3,2,1,0:T(8,128)(2,1)} %copy-done.1, bf16[4,3,256,640]{3,2,1,0:T(8,128)(2,1)S(1)} %get-tuple-element.8.c_ref), custom_call_target="tpu_custom_call" | custom-call | tf_op jit(solution)/shard_map/pallas_call | solution.py:275
  (2 shorter events, 0.0 us)
Async XLA Ops:
  0.0 3.1 %copy-start = (f32[512,256]{1,0:T(8,128)S(1)}, f32[512,256]{1,0:T(8,128)}, u32[]{:S(2)}) copy-start(f32[512,256]{1,0:T(8,128)} %param.5) | copy-start | bytes 1572868
  0.8 3.4 %copy-start.3 = (f32[2560,256]{1,0:T(8,128)S(1)}, f32[2560,256]{1,0:T(8,128)}, u32[]{:S(2)}) copy-start(f32[2560,256]{1,0:T(8,128)} %param.4) | copy-start | bytes 7864324
  6.8 101.2 %copy-start.2 = (s32[129,2]{0,1:T(2,128)S(1)}, s32[129,2]{0,1:T(2,128)}, u32[]{:S(2)}) copy-start(s32[129,2]{0,1:T(2,128)} %param.7) | copy-start | bytes 3100
  101.0 7.0 %copy-start.1 = (bf16[4,16,256,640]{3,2,1,0:T(8,128)(2,1)}, bf16[4,16,256,640]{3,2,1,0:T(8,128)(2,1)S(1)}, u32[]{:S(2)}) copy-start(bf16[4,16,256,640]{3,2,1,0:T(8,128)(2,1)S(1)} %get-tuple-element.7.r_ref) | copy-start | bytes 62914564

commit v3 on v2

v3 whole, which is shorter than its diff:
```python
import functools
import heapq
import math

import jax
import jax.numpy as jnp
from jax import lax
from jax.experimental import pallas as pl
from jax.experimental.pallas import tpu as pltpu
from jax.sharding import PartitionSpec as P

F = 1024
M = 16384
MB = 128
N_SA = 4
N_ROW = 4
N_COL = 16
N_Z = 8
QUART = MB // N_SA
CENT = 256
COUNT = 640
SPLIT = 384
ALL_ROWS = (0, CENT)
LOW_ROWS = (0, CENT // 2)
HIGH_ROWS = (CENT // 2, CENT)
ALL_COLS = (0, COUNT)
Z_FIRST = (0, SPLIT)
Y_FIRST = (SPLIT, COUNT)


class Send:
    def __init__(self, link, src, dst, rows, cols, deps, rank):
        self.link, self.src, self.dst, self.rows, self.cols = link, src, dst, rows, cols
        self.deps, self.rank = deps, rank

    def size(self):
        return 2 * (self.rows[1] - self.rows[0]) * (self.cols[1] - self.cols[0])


def spread_plan():
    sends = []

    def add(*args):
        sends.append(Send(*args))
        return len(sends) - 1

    def ring(axis, size, slot_of, start, cols, deps, rank):
        filled = {}
        for sign, half in (("+", LOW_ROWS), ("-", HIGH_ROWS)):
            step = -1 if sign == "+" else 1
            need, at = deps, start
            for hop in range(1, size // 2 + 1):
                rows = half if hop == size // 2 else ALL_ROWS
                to = (at + step) % size
                k = add(axis + sign, slot_of(at), slot_of(to), rows, cols, need, rank + hop)
                filled.setdefault(to, []).append(k)
                need, at = [k], to
        return filled

    y_own = ring("y", N_SA, lambda d: ("R", d, 0, 0), 0, ALL_COLS, [], 0)
    z_own = ring("z", N_Z, lambda d: ("R", 0, d, 0), 0, Z_FIRST, [], 0)
    arrived = {}
    for dz in range(1, N_Z):
        arrived[0, dz, Z_FIRST] = z_own[dz]
        got = ring("y", N_SA, lambda d: ("R", d, dz, 0), 0, Z_FIRST, z_own[dz], 10)
        for dy in range(1, N_SA):
            arrived[dy, dz, Z_FIRST] = got[dy]
    for dy in range(N_SA):
        need = y_own[dy] if dy else []
        got = ring("z", N_Z, lambda d: ("R", dy, d, 0), 0, Y_FIRST, need, 10)
        for dz in range(1, N_Z):
            arrived[dy, dz, Y_FIRST] = got[dz]
        ring("x", N_ROW, lambda d: ("C", dy, d) if d else ("R", dy, 0, 0), 0, ALL_COLS, need, 20)
        add("s", ("R", dy, 0, 0), ("R", dy, 0, 1), ALL_ROWS, ALL_COLS, need, 30)
    for (dy, dz, cols), need in arrived.items():
        add("s", ("R", dy, dz, 0), ("R", dy, dz, 1), ALL_ROWS, cols, need, 30)
    return sends


def spread_order(sends):
    rate = {"s": 200e3}
    free, pending, done, events, queue = {}, set(range(len(sends))), set(), [], []

    def start_ready(now):
        ready = sorted((k for k in pending if all(d in done for d in sends[k].deps)), key=lambda k: (sends[k].rank, k))
        for k in ready:
            pending.discard(k)
            link = sends[k].link
            begin = max(now, free.get(link, 0.0))
            free[link] = begin + sends[k].size() / rate.get(link, 46e3)
            heapq.heappush(queue, (free[link] + 1.7, k))
        return ready

    events.append((None, start_ready(0.0)))
    while queue:
        now, k = heapq.heappop(queue)
        done.add(k)
        events.append((k, start_ready(now)))
    return events, max(free.values())


def slot_of(place):
    return place[2] * 2 + place[3]


def left_place(dev, half, slot, slot_half):
    return (dev * 2 + half) * 2 * N_COL + slot * 2 + slot_half


def right_place(slot, half, place):
    return 2 * N_ROW * 2 * N_COL + (slot * 2 + half) * 2 * N_ROW + place


def table_places(table, x, col):
    i, j = table[:, 0], table[:, 1]
    row_i, col_i, half_i = i // (2 * N_COL), (i // 2) % N_COL, i % 2
    row_j, col_j, half_j = j // (2 * N_COL), (j // 2) % N_COL, j % 2

    def far_col(c):
        return (c // 2 - col // 2 + N_Z) % N_Z * 2 + (c + col) % 2

    def far_row(r):
        return (r - x + N_ROW) % N_ROW

    straight = jnp.logical_and(row_i == x, col_j == col)
    left = left_place(far_row(row_j), half_j, far_col(col_i), half_i)
    right = right_place(far_col(col_j), half_j, far_row(row_i) * 2 + half_i)
    return jnp.where(straight, left, right).astype(jnp.int32)


def compute_plan(sends, events):
    left_r, left_c = {}, 0
    for send in sends:
        if send.dst[0] == "R":
            left_r[slot_of(send.dst)] = left_r.get(slot_of(send.dst), 0) + 1
        else:
            left_c += 1
    ready, group, plan, waiting = [], [], [], []
    for arrival, _ in events:
        if arrival is not None:
            send = sends[arrival]
            if send.dst[0] == "C":
                left_c -= 1
                if left_c == 0:
                    ready.append(("columns", None))
                    ready.extend(waiting)
                    waiting = []
            else:
                slot = slot_of(send.dst)
                left_r[slot] -= 1
                if left_r[slot] == 0:
                    todo = [("right", slot)]
                    group.append(slot)
                    if len(group) == 4:
                        todo.append(("rows", tuple(group)))
                        todo.extend(("left", (tuple(group), dev)) for dev in range(N_ROW))
                        group = []
                    if left_c:
                        waiting.extend(todo)
                    else:
                        ready.extend(todo)
        plan.append([ready.pop(0)] if ready else [])
    plan[-1].extend(ready)
    return plan


def spread_kernel(sends, events, plan, place_of, part, o_ref, r_all, c_all, blocks, rq, cq, from_low, from_high, merge,
                  rs_send, rs_recv, out_sems, in_sems):
    y, x, col = lax.axis_index("sa"), lax.axis_index("row"), lax.axis_index("col")
    z, core = col // 2, col % 2
    yp, yo, ym = (y + 1) % N_SA, (y + 2) % N_SA, (y + 3) % N_SA
    to = {
        "y+": {"sa": yp},
        "y-": {"sa": ym},
        "x+": {"row": (x + 1) % N_ROW},
        "x-": {"row": (x + 3) % N_ROW},
        "z+": {"col": (z + 1) % N_Z * 2 + core},
        "z-": {"col": (z + 7) % N_Z * 2 + core},
        "s": {"col": z * 2 + 1 - core},
    }
    mesh_id = pl.DeviceIdType.MESH
    barrier = pltpu.get_barrier_semaphore()
    for peer in to.values():
        pl.semaphore_signal(barrier, inc=1, device_id=peer, device_id_type=mesh_id)
    pl.semaphore_wait(barrier, len(to))

    low, high = pl.ds(0, CENT // 2), pl.ds(CENT // 2, CENT // 2)

    def rs(src, buf, slot, link):
        way = 0 if link == "y+" else 3
        copy = pltpu.make_async_remote_copy(
            src_ref=src, dst_ref=buf.at[slot], send_sem=rs_send.at[way + slot], recv_sem=rs_recv.at[way + slot],
            device_id=to[link], device_id_type=mesh_id)
        copy.start()
        return copy

    copies = [
        rs(part.at[yo, low], from_low, 0, "y+"),
        rs(part.at[yo, high], from_high, 0, "y-"),
        rs(part.at[yp, high], from_low, 1, "y+"),
        rs(part.at[ym, low], from_high, 1, "y-"),
    ]
    copies[0].wait_recv()
    merge[0] = part[yp, :CENT // 2] + from_low[0]
    copies.append(rs(merge.at[0], from_low, 2, "y+"))
    copies[1].wait_recv()
    merge[1] = part[ym, CENT // 2:] + from_high[0]
    copies.append(rs(merge.at[1], from_high, 2, "y-"))
    for k in range(2, 6):
        copies[k].wait_recv()
    low_sum = part[y, :CENT // 2] + from_low[2] + from_high[1]
    r_all[0, :CENT // 2, :COUNT] = jnp.exp((2.0 * F - low_sum) / (4.0 * math.sqrt(F))).astype(jnp.bfloat16)
    high_sum = part[y, CENT // 2:] + from_low[1] + from_high[2]
    r_all[0, CENT // 2:, :COUNT] = jnp.exp((2.0 * F - high_sum) / (4.0 * math.sqrt(F))).astype(jnp.bfloat16)
    for copy in copies:
        copy.wait_send()

    def place_ref(place, rows, cols):
        rows = pl.ds(rows[0], rows[1] - rows[0])
        cols = pl.ds(place[1] * COUNT + cols[0], cols[1] - cols[0])
        if place[0] == "R":
            return r_all.at[slot_of(place), rows, cols]
        return c_all.at[place[2] - 1, rows, cols]

    def column(dev):
        return c_all.at[dev - 1] if dev else r_all.at[0]

    def quarter(half):
        return pl.ds(pl.multiple_of(half * MB + y * QUART, QUART), QUART)

    def dot(left, right):
        return lax.dot_general(left, right, (((1,), (1,)), ((), ())), preferred_element_type=jnp.float32)

    def compute(kind, what):
        if kind == "columns":
            for dev in range(N_ROW):
                for half in range(2):
                    top = (dev * 2 + half) * QUART
                    cq[top:top + QUART, :] = column(dev)[quarter(half), :]
        elif kind == "rows":
            for n, slot in enumerate(what):
                for half in range(2):
                    top = (n * 2 + half) * QUART
                    rq[top:top + QUART, :] = r_all[slot, quarter(half), :]
        elif kind == "right":
            got = dot(cq[...], r_all[what])
            for half in range(2):
                for n in range(2 * N_ROW):
                    blocks[right_place(what, half, n)] = got[n * QUART:(n + 1) * QUART, half * MB:(half + 1) * MB]
        else:
            slots, dev = what
            got = dot(rq[...], column(dev)[...])
            for half in range(2):
                for n in range(8):
                    blocks[left_place(dev, half, slots[n // 2], n % 2)] = got[
                        n * QUART:(n + 1) * QUART, half * MB:(half + 1) * MB]

    started = []
    for k, send in enumerate(sends):
        started.append(pltpu.make_async_remote_copy(
            src_ref=place_ref(send.src, send.rows, send.cols), dst_ref=place_ref(send.dst, send.rows, send.cols),
            send_sem=out_sems.at[k], recv_sem=in_sems.at[k], device_id=to[send.link], device_id_type=mesh_id))
    for (arrival, ready), tasks in zip(events, plan):
        if arrival is not None:
            started[arrival].wait_recv()
        for k in ready:
            started[k].start()
        for task in tasks:
            compute(*task)
    for copy in started:
        copy.wait_send()

    @pl.loop(0, o_ref.shape[0] // 3)
    def _(step):
        for n in range(3):
            k = step * 3 + n
            o_ref[k] = blocks[place_of[k]] * (1.0 / (N_SA * COUNT))


def spread(place_of, part):
    sends = spread_plan()
    events, _ = spread_order(sends)
    half = (CENT // 2, COUNT)
    whole = N_SA * COUNT
    vmem = pl.BlockSpec(memory_space=pltpu.VMEM)
    return pl.pallas_call(
        functools.partial(spread_kernel, sends, events, compute_plan(sends, events)),
        out_shape=jax.ShapeDtypeStruct((place_of.shape[0], QUART, MB), jnp.float32),
        in_specs=[pl.BlockSpec(memory_space=pltpu.SMEM), vmem],
        out_specs=vmem,
        scratch_shapes=[
            pltpu.VMEM((N_COL, CENT, whole), jnp.bfloat16),
            pltpu.VMEM((N_ROW - 1, CENT, whole), jnp.bfloat16),
            pltpu.VMEM((2 * 2 * N_ROW * 2 * N_COL, QUART, MB), jnp.float32),
            pltpu.VMEM((CENT, whole), jnp.bfloat16),
            pltpu.VMEM((CENT, whole), jnp.bfloat16),
            pltpu.VMEM((3, *half), jnp.float32),
            pltpu.VMEM((3, *half), jnp.float32),
            pltpu.VMEM((2, *half), jnp.float32),
            pltpu.SemaphoreType.DMA((6,)),
            pltpu.SemaphoreType.DMA((6,)),
            pltpu.SemaphoreType.DMA((len(sends),)),
            pltpu.SemaphoreType.DMA((len(sends),)),
        ],
        compiler_params=pltpu.CompilerParams(
            collective_id=0, has_side_effects=True, vmem_limit_bytes=52 * 2**20
        ),
    )(place_of, part)


def partial_distance(states, centres):
    parts = states.reshape(N_SA, states.shape[0] // N_SA, states.shape[1])
    inner = jnp.einsum(
        "cf,qsf->qcs", centres, parts, precision=lax.Precision.HIGHEST, preferred_element_type=jnp.float32
    )
    sample_norms = jnp.sum(parts * parts, axis=2)[:, None, :]
    centre_norms = jnp.sum(centres * centres, axis=1)[None, :, None]
    return sample_norms + centre_norms - 2.0 * inner


def shards(states, pool, pick, tile_table):
    row, col = lax.axis_index("row"), lax.axis_index("col")
    local = pick - (row * N_COL + col) * pool.shape[0]
    centres = pool.at[local].get(mode="promise_in_bounds")
    return spread(table_places(tile_table, row, col), partial_distance(states, centres))


def solution(mesh):
    placed = (P(None, "sa"), P(("row", "col"), "sa"), P(("row", "col")), P(("row", "col"), None))
    return jax.shard_map(
        shards, mesh=mesh, in_specs=placed, out_specs=P(("row", "col"), "sa", None), check_vma=False
    )
```

time: 151 us -> 124 us (0.82)
  Pallas kernels: 137 us -> 112 us
  local copies, waits for them, and re-layouts: 7.96 us -> 4.84 us
  matrix products: 2.52 us -> 4.03 us
    pallas_call x2 -> x1, Pallas kernels: 137 us -> 112 us  [spread(): pl.pallas_call(functools.partial(spread_kernel, sends, events, compute_pl...]
    unnamed x8 -> x5, local copies, waits for them, and re-layouts: 6.98 us -> 3.1 us
    dot_general x1, matrix products: 2.52 us -> 4.03 us  [partial_distance(): jnp.einsum('cf,qsf->qcs', centres, parts, precision=lax.Precision.HIGHEST...]
where the time goes in v3:
time: 124 us
  Pallas kernels  112 us (90%)
  local copies, waits for them, and re-layouts  4.84 us (4%)
  matrix products  4.03 us (3%)
  other arithmetic  3.21 us (3%)
    pallas_call x1, Pallas kernels, spread(): pl.pallas_call(functools.partial(spread_kernel, sends, events, compute_pl...  112 us
    dot_general x1, matrix products, partial_distance(): jnp.einsum('cf,qsf->qcs', centres, parts, precision=lax.Precision.HIGHEST...  4.03 us
    unnamed x5, local copies, waits for them, and re-layouts  3.1 us

profile of v3, /device:TPU:1, one launch (start us, length us, event | category | flops | bytes accessed | tf_op | source)
XLA Modules:
  0.0 124.2 jit_solution(1828982702657687365)
XLA Ops:
  0.0 0.0 copy-start
  0.0 0.7 compare_select_fusion
  0.7 0.8 fusion.18
  1.6 0.0 copy-start.1
  1.6 2.3 %multiply_reduce_fusion = f32[2560]{0:T(1024)S(1)} fusion(f32[2560,256]{1,0:T(8,128)} %param.4), kind=kLoop, calls=%fused_computation.2 | loop fusion | flops 1308160 | bytes 2631680 | tf_op jit(solution)/shard_map/reduce_sum | solution.py:316
  3.9 0.0 copy-done
  3.9 1.0 gather_fusion
  4.9 0.1 multiply_reduce_fusion.1
  5.0 0.0 copy-done.1
  5.0 4.0 %bitcast_subtract_fusion.part = f32[4,256,640]{2,1,0:T(8,128)} fusion(f32[4,640,256]{2,1,0:T(8,128)S(1)} %bitcast.9, f32[256]{0:T(256)S(1)} %multiply_reduce_fusion.1, f32[4,640]{1,0:T(4,128)S(1)} %add.149, f32[256,256]{1,0:T(8,128)S(1)} %gather_fusion), kind=kOutput, calls=%fused_computation.1 | convolution fusion | flops 2015232000 | bytes 5516288 | tf_op jit(solution)/shard_map/cf,qsf->qcs/dot_general | solution.py:313
  9.0 112.1 %shard_map.46 = f32[129,32,128]{2,1,0:T(8,128)} custom-call(s32[129]{0:T(256)S(1)} %and_select_fusion.13.place_of, f32[4,256,640]{2,1,0:T(8,128)} %bitcast_subtract_fusion.part), custom_call_target="tpu_custom_call" | custom-call | tf_op jit(solution)/shard_map/pallas_call | solution.py:286
  121.1 3.1 %copy.6 = f32[129,32,128]{2,1,0:T(8,128)} copy(f32[129,32,128]{2,1,0:T(8,128)} %shard_map.46) | data formatting | bytes 4227072
  (3 shorter events, 0.1 us)
Async XLA Ops:
  0.0 3.9 %copy-start = (f32[512,256]{1,0:T(8,128)S(1)}, f32[512,256]{1,0:T(8,128)}, u32[]{:S(2)}) copy-start(f32[512,256]{1,0:T(8,128)} %param.5) | copy-start | bytes 1572868
  1.6 3.4 %copy-start.1 = (f32[2560,256]{1,0:T(8,128)S(1)}, f32[2560,256]{1,0:T(8,128)}, u32[]{:S(2)}) copy-start(f32[2560,256]{1,0:T(8,128)} %param.4) | copy-start | bytes 7864324

commit v4 on v0

v4 whole, which is shorter than its diff:
```python
import functools
import heapq
import math

import jax
import jax.numpy as jnp
from jax import lax
from jax.experimental import pallas as pl
from jax.experimental.pallas import tpu as pltpu
from jax.sharding import PartitionSpec as P

F = 1024
M = 16384
MB = 128
N_SA = 4
N_ROW = 4
N_COL = 16
N_Z = 8
QUART = MB // N_SA
CENT = 256
COUNT = 640
POOL_DEV = 512
FEAT = F // N_SA
SHARE = COUNT // 8
SPLIT = 384
Z_FIRST = (0, SPLIT)
Y_FIRST = (SPLIT, COUNT)
EVERY = (0, COUNT)
GROUPS = ((0, 1, 2, 14), (3, 15, 4, 12), (5, 13, 6, 10), (7, 11, 8, 9))
RATE = {"s": 300e3}
LINK_RATE = 45e3
LATENCY = 1.7


class Send:
    def __init__(self, link, src, dst, size, deps, rank):
        self.link, self.src, self.dst, self.size = link, src, dst, size
        self.deps, self.rank = tuple(deps), rank


def ring(sends, axis, size, unit, own, halves, nbytes, deps, rank):
    filled = {}
    for sign, half in (("+", halves[0]), ("-", halves[1])):
        step = -1 if sign == "+" else 1
        need, at = deps, 0
        for hop in range(1, size // 2 + 1):
            last = hop == size // 2
            part = half if last else None
            to = (at + step) % size
            src = own(part) if at == 0 else unit(at, part)
            sends.append(Send(axis + sign, src, unit(to, part), nbytes // 2 if last else nbytes, need, rank + hop))
            filled.setdefault(to, []).append(len(sends) - 1)
            need, at = [len(sends) - 1], to
    return filled


def gather_inputs_plan():
    sends, tasks = [], []
    row_bytes = 4 * FEAT
    half = SHARE // 2

    def add(*args):
        sends.append(Send(*args))
        return len(sends) - 1

    relay = [add("y+", ("H", 2, 0, half), ("B", 0), half * row_bytes, (), 0),
             add("y-", ("H", 2, half, half), ("B", 1), half * row_bytes, (), 0)]
    come = {3: [add("y+", ("H", 1, 0, SHARE), ("S", 3, 0, 0, 0, SHARE), SHARE * row_bytes, (), 1)],
            1: [add("y-", ("H", 3, 0, SHARE), ("S", 1, 0, 0, 0, SHARE), SHARE * row_bytes, (), 1)]}
    come[2] = [add("y+", ("B", 0), ("S", 2, 0, 0, 0, half), half * row_bytes, relay[:1], 0),
               add("y-", ("B", 1), ("S", 2, 0, 0, half, half), half * row_bytes, relay[1:], 0)]

    def rows(part):
        return (0, SHARE) if part is None else part

    states = {}
    for d in (3, 1, 2):
        got = ring(sends, "x", N_ROW, lambda dx, part: ("S", d, dx, 0, *rows(part)),
                   lambda part: ("S", d, 0, 0, *rows(part)), ((0, half), (half, half)), SHARE * row_bytes, come[d], 0)
        got[0] = come[d]
        states[d] = [k for dx in range(N_ROW) for k in got[dx]]
        for dx in (0, 3, 1, 2):
            k = add("s", ("S", d, dx, 0, 0, SHARE), ("S", d, dx, 0, 0, SHARE), SHARE * row_bytes, got[dx], 5)
            states[d].append(k)

    def cent(part):
        return (0, CENT) if part is None else part

    halves = ((0, CENT // 2), (CENT // 2, CENT // 2))
    centres = ring(sends, "y", N_SA, lambda d, part: ("F", d, *cent(part)), lambda part: ("F", 0, *cent(part)), halves,
                   CENT * row_bytes, ("local", *relay), 3)
    tasks.append((("distance", 0), ("local",), 0.8))
    for d in (3, 1, 2):
        tasks.append((("distance", d), tuple(states[d] + centres[d]), 0.8))
    return sends, tasks


def spread_plan():
    sends = []

    def cut(cols, half):
        first, rows = (0, CENT) if half is None else half
        return (first, rows, cols[0], cols[1] - cols[0])

    halves = ((0, CENT // 2), (CENT // 2, CENT // 2))

    def area(cols):
        return 2 * CENT * (cols[1] - cols[0])

    def r_ring(axis, size, place, cols, deps, rank):
        return ring(sends, axis, size, lambda d, half: ("R", *place(d), 0, cut(cols, half)),
                    lambda half: ("R", *place(0), 0, cut(cols, half)), halves, area(cols), deps, rank)

    y_own = r_ring("y", N_SA, lambda d: (d, 0), EVERY, (), 0)
    z_own = r_ring("z", N_Z, lambda d: (0, d), Z_FIRST, (), 0)
    arrived = {}
    for dz in range(1, N_Z):
        arrived[0, dz, Z_FIRST] = z_own[dz]
        got = r_ring("y", N_SA, lambda d: (d, dz), Z_FIRST, z_own[dz], 10)
        for dy in range(1, N_SA):
            arrived[dy, dz, Z_FIRST] = got[dy]
    in_r, in_c = {(dy, 0): list(y_own[dy]) if dy else [] for dy in range(N_SA)}, {}
    for dy in range(N_SA):
        need = in_r[dy, 0]
        got = r_ring("z", N_Z, lambda d: (dy, d), Y_FIRST, need, 10)
        for dz in range(1, N_Z):
            arrived[dy, dz, Y_FIRST] = got[dz]
        got = ring(sends, "x", N_ROW, lambda d, half: ("C", dy, d, cut(EVERY, half)),
                   lambda half: ("R", dy, 0, 0, cut(EVERY, half)), halves, area(EVERY), need, 20)
        in_c[dy] = [k for ks in got.values() for k in ks] + need
        sends.append(Send("s", ("R", dy, 0, 0, cut(EVERY, None)), ("R", dy, 0, 1, cut(EVERY, None)), area(EVERY), need, 30))
        in_r[dy, 1] = [len(sends) - 1]
    for (dy, dz, cols), need in arrived.items():
        sends.append(Send("s", ("R", dy, dz, 0, cut(cols, None)), ("R", dy, dz, 1, cut(cols, None)), area(cols), need, 30))
        in_r.setdefault((dy, dz * 2), []).extend(need)
        in_r.setdefault((dy, dz * 2 + 1), []).append(len(sends) - 1)

    tasks = []
    for dy in range(N_SA):
        tasks.append((("columns", dy), tuple(in_c[dy]), 0.15))
    for group in GROUPS:
        for dy in range(N_SA):
            need = [k for slot in group for k in in_r[dy, slot]] + in_c[dy]
            tasks.append((("right", (group, dy)), tuple(need), 0.5))
            tasks.append((("left", (group, dy)), tuple(need), 0.5))
    return sends, tasks


def timetable(sends, tasks, local):
    free, pending, done, queue, steps = {}, set(range(len(sends))), set(), [], []
    undone = list(range(len(tasks)))

    def start_ready(now):
        ready = sorted((k for k in pending if all(d in done for d in sends[k].deps)), key=lambda k: (sends[k].rank, k))
        for k in ready:
            pending.discard(k)
            link = sends[k].link
            free[link] = max(now, free.get(link, 0.0)) + sends[k].size / RATE.get(link, LINK_RATE)
            heapq.heappush(queue, (free[link] + LATENCY, k))
            steps.append(("start", k))

    core = 0.0
    start_ready(core)
    if local is not None:
        core += local
        steps.append(("local", None))
        done.add("local")
        start_ready(core)
    while queue or undone:
        coming = queue[0][0] if queue else math.inf
        ready = [t for t in undone if all(d in done for d in tasks[t][1])]
        if ready and coming - core >= 0.6 * tasks[ready[0]][2]:
            undone.remove(ready[0])
            core += tasks[ready[0]][2]
            steps.append(("task", tasks[ready[0]][0]))
            continue
        now, k = heapq.heappop(queue)
        core = max(core, now)
        done.add(k)
        steps.append(("wait", k))
        start_ready(core)
    return steps, core


def left_place(dev, half, slot, slot_half):
    return (dev * 2 + half) * 2 * N_COL + slot * 2 + slot_half


def right_place(slot, half, place):
    return 2 * N_ROW * 2 * N_COL + (slot * 2 + half) * 2 * N_ROW + place


def normal_kernel(plans, steps, table, pick, states, pool, o_ref, r_all, c_all, blocks, cq, rq, s_all, f_all, relay,
                  pool_local, inner, sample_norms, centre_norms, place_of, copy_sems, first_out, first_in, out_sems,
                  in_sems):
    y, x, col = lax.axis_index("sa"), lax.axis_index("row"), lax.axis_index("col")
    z, core = col // 2, col % 2
    to = {
        "y+": {"sa": (y + 1) % N_SA},
        "y-": {"sa": (y + 3) % N_SA},
        "x+": {"row": (x + 1) % N_ROW},
        "x-": {"row": (x + 3) % N_ROW},
        "z+": {"col": (z + 1) % N_Z * 2 + core},
        "z-": {"col": (z + 7) % N_Z * 2 + core},
        "s": {"col": z * 2 + 1 - core},
    }
    mesh_id = pl.DeviceIdType.MESH
    pool_copy = pltpu.make_async_copy(pool, pool_local, copy_sems.at[0])
    pool_copy.start()
    states_copy = pltpu.make_async_copy(
        states.at[pl.ds(pl.multiple_of(y * COUNT, COUNT), COUNT), :], s_all.at[0], copy_sems.at[1])
    states_copy.start()
    barrier = pltpu.get_barrier_semaphore()
    for peer in to.values():
        pl.semaphore_signal(barrier, inc=1, device_id=peer, device_id_type=mesh_id)
    pl.semaphore_wait(barrier, len(to))

    def place_ref(place):
        kind = place[0]
        if kind == "H":
            first = (y + place[1]) % N_SA * COUNT + (x * 2 + core) * SHARE + place[2]
            return states.at[pl.ds(pl.multiple_of(first, 8), place[3]), :]
        if kind == "B":
            return relay.at[place[1]]
        if kind == "S":
            first = ((x + place[2]) % N_ROW * 2 + core) * SHARE + place[4]
            return s_all.at[place[1], pl.ds(pl.multiple_of(first, 8), place[5]), :]
        if kind == "F":
            return f_all.at[place[1], pl.ds(place[2], place[3]), :]
        first, rows, start, count = place[-1]
        rows, cols = pl.ds(first, rows), pl.ds(place[1] * COUNT + start, count)
        if kind == "R":
            return r_all.at[place[2] * 2 + place[3], rows, cols]
        return c_all.at[place[2] - 1, rows, cols]

    def landing(send):
        if send.src[0] == "S":
            return place_ref(send.src)
        return place_ref(send.dst)

    def copies_of(sends, out, into):
        return [
            pltpu.make_async_remote_copy(
                src_ref=place_ref(send.src), dst_ref=landing(send), send_sem=out.at[k], recv_sem=into.at[k],
                device_id=to[send.link], device_id_type=mesh_id)
            for k, send in enumerate(sends)
        ]

    def dot(left, right, precision=None):
        return lax.dot_general(left, right, (((1,), (1,)), ((), ())), precision=precision,
                               preferred_element_type=jnp.float32)

    def distance(d):
        sample, centre = s_all[d], f_all[d]
        cross = dot(centre, sample, lax.Precision.HIGHEST)
        norms = dot(jnp.ones((8, FEAT), jnp.float32), sample * sample, lax.Precision.HIGHEST)
        own = jnp.sum(centre * centre, axis=1, keepdims=True)
        if d:
            inner[...] += cross
            sample_norms[...] += norms
            centre_norms[...] += own
        else:
            inner[...], sample_norms[...], centre_norms[...] = cross, norms, own

    def local():
        pool_copy.wait()

        @pl.loop(0, CENT // 8)
        def _(m):
            for n in range(8):
                f_all[0, m * 8 + n] = pool_local[pick[m * 8 + n] & (POOL_DEV - 1)]

        states_copy.wait()

    def column(dev):
        return c_all.at[dev - 1] if dev else r_all.at[0]

    def quarter(half):
        return pl.ds(pl.multiple_of(half * MB + y * QUART, QUART), QUART)

    begun = set()

    def put(where, value, key):
        if key in begun:
            blocks[where] += value
        else:
            blocks[where] = value

    def task(kind, what):
        if kind == "distance":
            distance(what)
            return
        if kind == "columns":
            cols = slice(what * COUNT, (what + 1) * COUNT)
            for dev in range(N_ROW):
                for half in range(2):
                    top = (dev * 2 + half) * QUART
                    cq[top:top + QUART, cols] = column(dev)[quarter(half), cols]
            return
        group, dy = what
        cols = slice(dy * COUNT, (dy + 1) * COUNT)
        if kind == "right":
            for slot in group:
                got = dot(cq[:, cols], r_all[slot, :, cols])
                for half in range(2):
                    for n in range(2 * N_ROW):
                        put(right_place(slot, half, n), got[n * QUART:(n + 1) * QUART, half * MB:(half + 1) * MB],
                            (kind, group))
        else:
            for n, slot in enumerate(group):
                for half in range(2):
                    top = (n * 2 + half) * QUART
                    rq[top:top + QUART, :] = r_all[slot, quarter(half), cols]
            for dev in range(N_ROW):
                got = dot(rq[...], column(dev)[:, cols])
                for half in range(2):
                    for n in range(8):
                        put(left_place(dev, half, group[n // 2], n % 2),
                            got[n * QUART:(n + 1) * QUART, half * MB:(half + 1) * MB], (kind, group))
        begun.add((kind, group))

    def run(copies, order):
        for kind, what in order:
            if kind == "wait":
                copies[what].wait_recv()
            elif kind == "start":
                copies[what].start()
            elif kind == "local":
                local()
            else:
                task(*what)

    first = copies_of(plans[0], first_out, first_in)
    run(first, steps[0])
    total = sample_norms[:1, :] + centre_norms[...] - 2.0 * inner[...]
    r_all[0, :, :COUNT] = jnp.exp((2.0 * F - total) / (4.0 * math.sqrt(F))).astype(jnp.bfloat16)
    second = copies_of(plans[1], out_sems, in_sems)
    for kind, what in steps[1]:
        if kind != "start":
            break
        second[what].start()
    for copy in first:
        copy.wait_send()

    @pl.loop(0, o_ref.shape[0] // 3)
    def _(m):
        for n in range(3):
            k = m * 3 + n
            i, j = table[0, k], table[1, k]
            row_i, col_i, half_i = i >> 5, (i >> 1) & 15, i & 1
            row_j, col_j, half_j = j >> 5, (j >> 1) & 15, j & 1

            def far_col(c):
                return (((c >> 1) - z) & 7) * 2 + ((c + core) & 1)

            left = left_place((row_j - x) & 3, half_j, far_col(col_i), half_i)
            right = right_place(far_col(col_j), half_j, ((row_i - x) & 3) * 2 + half_i)
            straight = jnp.logical_and(row_i == x, col_j == col)
            place_of[k] = right + (left - right) * straight.astype(jnp.int32)

    begin = [k for k, (kind, _) in enumerate(steps[1]) if kind != "start"][0]
    run(second, steps[1][begin:])
    for copy in second:
        copy.wait_send()

    @pl.loop(0, o_ref.shape[0] // 3)
    def _(m):
        for n in range(3):
            k = m * 3 + n
            o_ref[k] = blocks[place_of[k]] * (1.0 / (N_SA * COUNT))


def normal_tiles(table, pick, states, pool):
    first, first_tasks = gather_inputs_plan()
    second, second_tasks = spread_plan()
    steps = [timetable(first, first_tasks, 1.5)[0], timetable(second, second_tasks, None)[0]]
    whole = N_SA * COUNT
    smem, anywhere = pl.BlockSpec(memory_space=pltpu.SMEM), pl.BlockSpec(memory_space=pl.ANY)
    return pl.pallas_call(
        functools.partial(normal_kernel, [first, second], steps),
        out_shape=jax.ShapeDtypeStruct((table.shape[1], QUART, MB), jnp.float32),
        in_specs=[smem, smem, anywhere, anywhere],
        out_specs=pl.BlockSpec(memory_space=pltpu.VMEM),
        scratch_shapes=[
            pltpu.VMEM((N_COL, CENT, whole), jnp.bfloat16),
            pltpu.VMEM((N_ROW - 1, CENT, whole), jnp.bfloat16),
            pltpu.VMEM((2 * 2 * N_ROW * 2 * N_COL, QUART, MB), jnp.float32),
            pltpu.VMEM((CENT, whole), jnp.bfloat16),
            pltpu.VMEM((CENT, COUNT), jnp.bfloat16),
            pltpu.VMEM((N_SA, COUNT, FEAT), jnp.float32),
            pltpu.VMEM((N_SA, CENT, FEAT), jnp.float32),
            pltpu.VMEM((2, SHARE // 2, FEAT), jnp.float32),
            pltpu.VMEM(pool.shape, jnp.float32),
            pltpu.VMEM((CENT, COUNT), jnp.float32),
            pltpu.VMEM((8, COUNT), jnp.float32),
            pltpu.VMEM((CENT, 1), jnp.float32),
            pltpu.SMEM((table.shape[1],), jnp.int32),
            pltpu.SemaphoreType.DMA((2,)),
            pltpu.SemaphoreType.DMA((len(first),)),
            pltpu.SemaphoreType.DMA((len(first),)),
            pltpu.SemaphoreType.DMA((len(second),)),
            pltpu.SemaphoreType.DMA((len(second),)),
        ],
        compiler_params=pltpu.CompilerParams(
            collective_id=0, has_side_effects=True, vmem_limit_bytes=56 * 2**20
        ),
    )(table, pick, states, pool)


def shards(states, pool, pick, tile_table):
    return normal_tiles(tile_table.T, pick, states, pool)


def solution(mesh):
    placed = (P(None, "sa"), P(("row", "col"), "sa"), P(("row", "col")), P(("row", "col"), None))
    return jax.shard_map(
        shards, mesh=mesh, in_specs=placed, out_specs=P(("row", "col"), "sa", None), check_vma=False
    )
```

time: 392 us -> 99.1 us (0.25)
  waiting for transfers between devices: 230 us -> 0 us
  local copies, waits for them, and re-layouts: 106 us -> 3.09 us
  Pallas kernels: 0 us -> 95.9 us
  matrix products: 33.6 us -> 0 us
  between operations: 13.2 us -> 0.01 us
  starting transfers between devices: 5.23 us -> 0 us
    all_gather x2 -> x0, waiting for transfers between devices: 150 us -> none  [the longest x1 113 us: shards(): kernel_panel = lax.all_gather(kernel, ('row', 'col'), axis=1, tiled=True)]
    pallas_call x0 -> x1, Pallas kernels: none -> 95.9 us  [normal_tiles(): pl.pallas_call(functools.partial(normal_kernel, [first, second], steps),...]
    reduce_scatter x1 -> x0, waiting for transfers between devices: 80.5 us -> none  [shards(): lax.psum_scatter(partial_tiles, 'sa', scatter_dimension=1, tiled=True)]
    gather x7 -> x0, local copies, waits for them, and re-layouts: 75.5 us -> none  [the longest x3 37.3 us: products(): right_blocks = jnp.take(panel_blocks, tile_pairs[:, 1], axis=1)]
    dot_general x4 -> x0, matrix products: 33.6 us -> none  [the longest x3 28 us: products(): jnp.einsum('sga,sgb->gab', left_blocks, right_blocks, preferred_element_t...]
    while x1 -> x0, local copies, waits for them, and re-layouts: 28.2 us -> none  [shards(): partial_tiles = lax.map(products, tile_groups).reshape(tile_count, MB, MB)]
    all_to_all x1 -> x0, starting transfers between devices: 5.14 us -> none  [shards(): lax.all_to_all(states, 'sa', split_axis=0, concat_axis=1, tiled=True)]
  transfers between devices with their start and end apart: 4 -> 0, of which waited for: 3 -> 0; matrix products, arithmetic and copies ran while one was open for 1% -> 0% of each run, Pallas kernels for 0% -> 0%
where the time goes in v4:
time: 99.1 us; the launch traced here: 99 us
  Pallas kernels  95.9 us (97%)
  local copies, waits for them, and re-layouts  3.09 us (3%)
    pallas_call x1, Pallas kernels, normal_tiles(): pl.pallas_call(functools.partial(normal_kernel, [first, second], steps),...  95.9 us
    unnamed x1, local copies, waits for them, and re-layouts  3.09 us

profile of v4, /device:TPU:1, one launch (start us, length us, event | category | flops | bytes accessed | tf_op | source)
XLA Modules:
  0.0 99.0 jit_solution(15621219156164490554)
XLA Ops:
  0.0 95.9 %shard_map.46 = f32[129,32,128]{2,1,0:T(8,128)} custom-call(s32[2,129]{1,0:T(2,128)} %bitcast.1, s32[256]{0:T(256)} %pick.1, f32[2560,256]{1,0:T(8,128)} %states.1, f32[512,256]{1,0:T(8,128)} %pool.1), custom_call_target="tpu_custom_call" | custom-call | tf_op jit(solution)/shard_map/pallas_call | solution.py:379
  95.9 3.1 %copy.6 = f32[129,32,128]{2,1,0:T(8,128)} copy(f32[129,32,128]{2,1,0:T(8,128)} %shard_map.46) | data formatting | bytes 4227072

commit v5 on v4

v5 whole, which is shorter than its diff:
```python
import functools
import heapq
import math

import jax
import jax.numpy as jnp
from jax import lax
from jax.experimental import pallas as pl
from jax.experimental.pallas import tpu as pltpu
from jax.sharding import PartitionSpec as P

F = 1024
M = 16384
MB = 128
N_SA = 4
N_ROW = 4
N_COL = 16
N_Z = 8
QUART = MB // N_SA
CENT = 256
COUNT = 640
POOL_DEV = 512
FEAT = F // N_SA
SPLIT = 384
Z_FIRST = (0, SPLIT)
Y_FIRST = (SPLIT, COUNT)
EVERY = (0, COUNT)
WINDOWS = (Z_FIRST, Y_FIRST)
PIECES = 3
GROUPS = ((0, 1, 2, 14), (3, 15, 4, 12), (5, 13, 6, 10), (7, 11, 8, 9))
RATE = {"s": 300e3}
LINK_RATE = 45e3
LATENCY = 1.7


class Send:
    def __init__(self, link, src, dst, size, deps, rank):
        self.link, self.src, self.dst, self.size = link, src, dst, size
        self.deps, self.rank = tuple(deps), rank


def ring(sends, axis, size, unit, own, halves, nbytes, deps, rank):
    filled = {}
    for sign, half in (("+", halves[0]), ("-", halves[1])):
        step = -1 if sign == "+" else 1
        need, at = deps, 0
        for hop in range(1, size // 2 + 1):
            last = hop == size // 2
            part = half if last else None
            to = (at + step) % size
            src = own(part) if at == 0 else unit(at, part)
            sends.append(Send(axis + sign, src, unit(to, part), nbytes // 2 if last else nbytes, need, rank + hop))
            filled.setdefault(to, []).append(len(sends) - 1)
            need, at = [len(sends) - 1], to
    return filled


def share_of(w):
    return (WINDOWS[w][1] - WINDOWS[w][0]) // 8


def inputs_plan(sends, tasks):
    row_bytes = 4 * FEAT

    def add(*args):
        sends.append(Send(*args))
        return len(sends) - 1

    relays = []
    for w in range(2):
        half = share_of(w) // 2
        need = ("local", *relays) if w else ()
        relays.append(add("y+", ("H", 2, w, 0, half), ("B", 2 * w, half), half * row_bytes, need, 4 * w))
        relays.append(add("y-", ("H", 2, w, half, half), ("B", 2 * w + 1, half), half * row_bytes, need, 4 * w))
    states, late = {}, ((), ("local", *relays[:2]))
    for w in range(2):
        share = share_of(w)
        half = share // 2
        come = {3: [add("y+", ("H", 1, w, 0, share), ("S", 3, 0, w, 0, share), share * row_bytes, late[w], 1 + 4 * w)],
                1: [add("y-", ("H", 3, w, 0, share), ("S", 1, 0, w, 0, share), share * row_bytes, late[w], 1 + 4 * w)]}
        come[2] = [add("y+", ("B", 2 * w, half), ("S", 2, 0, w, 0, half), half * row_bytes, [relays[2 * w]], 0),
                   add("y-", ("B", 2 * w + 1, half), ("S", 2, 0, w, half, half), half * row_bytes, [relays[2 * w + 1]], 0)]

        def rows(part):
            return (0, share) if part is None else part

        for d in (3, 1, 2):
            got = ring(sends, "x", N_ROW, lambda dx, part: ("S", d, dx, w, *rows(part)),
                       lambda part: ("S", d, 0, w, *rows(part)), ((0, half), (half, half)), share * row_bytes, come[d], 0)
            got[0] = come[d]
            states[d, w] = [k for dx in range(N_ROW) for k in got[dx]]
            for dx in (0, 3, 1, 2):
                place = ("S", d, dx, w, 0, share)
                states[d, w].append(add("s", place, place, share * row_bytes, got[dx], 5))

    def cent(part):
        return (0, CENT) if part is None else part

    halves = ((0, CENT // 2), (CENT // 2, CENT // 2))
    centres = ring(sends, "y", N_SA, lambda d, part: ("F", d, *cent(part)), lambda part: ("F", 0, *cent(part)), halves,
                   CENT * row_bytes, ("local", *relays[:2]), 3)
    tasks.append(("local", None, (), 1.5, True))
    for w in range(2):
        tasks.append(("distance", (0, w), ("local",), 0.5, False))
    for n in range(PIECES):
        tasks.append(("places", n, ("local",), 0.8, False))
    for w in range(2):
        for d in (3, 1, 2):
            tasks.append(("distance", (d, w), tuple(states[d, w] + centres[d]), 0.5, True))
        tasks.append(("kernel", w, tuple(("distance", (d, w)) for d in range(N_SA)), 0.3, True))


def spread_plan(sends, tasks):
    kernels = [("kernel", w) for w in range(2)]

    def cut(cols, half):
        first, rows = (0, CENT) if half is None else half
        return (first, rows, cols[0], cols[1] - cols[0])

    halves = ((0, CENT // 2), (CENT // 2, CENT // 2))

    def area(cols):
        return 2 * CENT * (cols[1] - cols[0])

    def r_ring(axis, size, place, cols, deps, rank):
        return ring(sends, axis, size, lambda d, half: ("R", *place(d), 0, cut(cols, half)),
                    lambda half: ("R", *place(0), 0, cut(cols, half)), halves, area(cols), deps, rank)

    z_own = r_ring("z", N_Z, lambda d: (0, d), Z_FIRST, kernels[:1], 6)
    y_own = [r_ring("y", N_SA, lambda d: (d, 0), WINDOWS[w], kernels[w:w + 1], 6) for w in range(2)]
    arrived = {}
    for dz in range(1, N_Z):
        arrived[0, dz, Z_FIRST] = z_own[dz]
        got = r_ring("y", N_SA, lambda d: (d, dz), Z_FIRST, z_own[dz], 10)
        for dy in range(1, N_SA):
            arrived[dy, dz, Z_FIRST] = got[dy]
    in_r, in_c = {(dy, 0): y_own[0][dy] + y_own[1][dy] if dy else kernels for dy in range(N_SA)}, {}
    for dy in range(N_SA):
        need = in_r[dy, 0]
        got = r_ring("z", N_Z, lambda d: (dy, d), Y_FIRST, y_own[1][dy] if dy else kernels[1:], 10)
        for dz in range(1, N_Z):
            arrived[dy, dz, Y_FIRST] = got[dz]
        got = ring(sends, "x", N_ROW, lambda d, half: ("C", dy, d, cut(EVERY, half)),
                   lambda half: ("R", dy, 0, 0, cut(EVERY, half)), halves, area(EVERY), need, 20)
        in_c[dy] = [k for ks in got.values() for k in ks] + need
        sends.append(Send("s", ("R", dy, 0, 0, cut(EVERY, None)), ("R", dy, 0, 1, cut(EVERY, None)), area(EVERY), need, 30))
        in_r[dy, 1] = [len(sends) - 1]
    for (dy, dz, cols), need in arrived.items():
        sends.append(Send("s", ("R", dy, dz, 0, cut(cols, None)), ("R", dy, dz, 1, cut(cols, None)), area(cols), need, 30))
        in_r.setdefault((dy, dz * 2), []).extend(need)
        in_r.setdefault((dy, dz * 2 + 1), []).append(len(sends) - 1)

    for dy in range(N_SA):
        tasks.append(("columns", dy, tuple(in_c[dy]), 0.15, False))
    for group in GROUPS:
        for dy in range(N_SA):
            need = [k for slot in group for k in in_r[dy, slot]] + in_c[dy]
            tasks.append(("right", (group, dy), (*need, ("columns", dy)), 0.5, False))
            tasks.append(("left", (group, dy), tuple(need), 0.5, False))


def timetable(sends, tasks):
    free, pending, done, queue, steps = {}, set(range(len(sends))), set(), [], []
    undone = list(range(len(tasks)))

    def start_ready(now):
        ready = sorted((k for k in pending if all(d in done for d in sends[k].deps)), key=lambda k: (sends[k].rank, k))
        for k in ready:
            pending.discard(k)
            link = sends[k].link
            free[link] = max(now, free.get(link, 0.0)) + sends[k].size / RATE.get(link, LINK_RATE)
            heapq.heappush(queue, (free[link] + LATENCY, k))
            steps.append(("start", k))

    core = 0.0
    start_ready(core)
    while queue or undone:
        coming = queue[0][0] if queue else math.inf
        ready = [t for t in undone if all(d in done for d in tasks[t][2])]
        ready.sort(key=lambda t: not tasks[t][4])
        if ready and coming - core >= (0.0 if tasks[ready[0]][4] else 0.6 * tasks[ready[0]][3]):
            kind, what, _, span, _ = tasks[ready[0]]
            undone.remove(ready[0])
            core += span
            steps.append((kind, what))
            done.add(kind if what is None else (kind, what))
            start_ready(core)
            continue
        now, k = heapq.heappop(queue)
        core = max(core, now)
        done.add(k)
        steps.append(("wait", k))
        start_ready(core)
    return steps, core


def left_place(dev, half, slot, slot_half):
    return (dev * 2 + half) * 2 * N_COL + slot * 2 + slot_half


def right_place(slot, half, place):
    return 2 * N_ROW * 2 * N_COL + (slot * 2 + half) * 2 * N_ROW + place


def normal_kernel(sends, steps, table, pick, states, pool, out, r_all, c_all, blocks, cq, rq, s_all, f_all, relay,
                  pool_local, inner, centre_norms, place_of, o_ref, copy_sems, out_sems, in_sems):
    y, x, col = lax.axis_index("sa"), lax.axis_index("row"), lax.axis_index("col")
    z, core = col // 2, col % 2
    to = {
        "y+": {"sa": (y + 1) % N_SA},
        "y-": {"sa": (y + 3) % N_SA},
        "x+": {"row": (x + 1) % N_ROW},
        "x-": {"row": (x + 3) % N_ROW},
        "z+": {"col": (z + 1) % N_Z * 2 + core},
        "z-": {"col": (z + 7) % N_Z * 2 + core},
        "s": {"col": z * 2 + 1 - core},
    }
    mesh_id = pl.DeviceIdType.MESH
    pool_copy = pltpu.make_async_copy(pool, pool_local, copy_sems.at[0])
    pool_copy.start()
    states_copy = pltpu.make_async_copy(
        states.at[pl.ds(pl.multiple_of(y * COUNT, COUNT), COUNT), :], s_all.at[0], copy_sems.at[1])
    states_copy.start()
    barrier = pltpu.get_barrier_semaphore()
    for peer in to.values():
        pl.semaphore_signal(barrier, inc=1, device_id=peer, device_id_type=mesh_id)
    pl.semaphore_wait(barrier, len(to))

    def place_ref(place):
        kind = place[0]
        if kind == "H":
            w = place[2]
            first = (y + place[1]) % N_SA * COUNT + WINDOWS[w][0] + (x * 2 + core) * share_of(w) + place[3]
            return states.at[pl.ds(pl.multiple_of(first, 8), place[4]), :]
        if kind == "B":
            return relay.at[place[1], pl.ds(0, place[2]), :]
        if kind == "S":
            w = place[3]
            first = WINDOWS[w][0] + ((x + place[2]) % N_ROW * 2 + core) * share_of(w) + place[4]
            return s_all.at[place[1], pl.ds(pl.multiple_of(first, 8), place[5]), :]
        if kind == "F":
            return f_all.at[place[1], pl.ds(place[2], place[3]), :]
        first, rows, start, count = place[-1]
        rows, cols = pl.ds(first, rows), pl.ds(place[1] * COUNT + start, count)
        if kind == "R":
            return r_all.at[place[2] * 2 + place[3], rows, cols]
        return c_all.at[place[2] - 1, rows, cols]

    def landing(send):
        if send.src[0] == "S":
            return place_ref(send.src)
        return place_ref(send.dst)

    copies = [
        pltpu.make_async_remote_copy(
            src_ref=place_ref(send.src), dst_ref=landing(send), send_sem=out_sems.at[k], recv_sem=in_sems.at[k],
            device_id=to[send.link], device_id_type=mesh_id)
        for k, send in enumerate(sends)
    ]

    def dot(left, right, precision=None):
        return lax.dot_general(left, right, (((1,), (1,)), ((), ())), precision=precision,
                               preferred_element_type=jnp.float32)

    begun = set()

    def put(ref, where, value, key):
        if key in begun:
            ref[where] += value
        else:
            ref[where] = value

    def distance(d, w):
        cols = slice(*WINDOWS[w])
        sample, centre = s_all[d, cols, :], f_all[d]
        squares = sample * sample
        squares = squares[:, :MB] + squares[:, MB:]
        norms = jnp.sum(squares.T, axis=0, keepdims=True)
        cross = dot(centre, sample, lax.Precision.HIGHEST)
        put(inner, (slice(None), cols), norms - 2.0 * cross, w)
        begun.add(w)
        if ("centre", d) not in begun:
            own = jnp.sum(centre * centre, axis=1, keepdims=True)
            put(centre_norms, (slice(None), slice(None)), own, "centres")
            begun.update(("centres", ("centre", d)))

    def kernel_values(w):
        cols = slice(*WINDOWS[w])
        total = inner[:, cols] + centre_norms[...]
        r_all[0, :, cols] = jnp.exp((2.0 * F - total) / (4.0 * math.sqrt(F))).astype(jnp.bfloat16)

    def places(piece):
        size = out.shape[0] // PIECES

        @pl.loop(0, size)
        def _(m):
            k = piece * size + m
            i, j = table[0, k], table[1, k]
            row_i, col_i, half_i = i >> 5, (i >> 1) & 15, i & 1
            row_j, col_j, half_j = j >> 5, (j >> 1) & 15, j & 1

            def far_col(c):
                return (((c >> 1) - z) & 7) * 2 + ((c + core) & 1)

            left = left_place((row_j - x) & 3, half_j, far_col(col_i), half_i)
            right = right_place(far_col(col_j), half_j, ((row_i - x) & 3) * 2 + half_i)
            straight = jnp.logical_and(row_i == x, col_j == col)
            place_of[k] = right + (left - right) * straight.astype(jnp.int32)

    def local():
        pool_copy.wait()

        @pl.loop(0, CENT // 8)
        def _(m):
            for n in range(8):
                f_all[0, m * 8 + n] = pool_local[pick[m * 8 + n] & (POOL_DEV - 1)]

        states_copy.wait()

    def column(dev):
        return c_all.at[dev - 1] if dev else r_all.at[0]

    def quarter(half):
        return pl.ds(pl.multiple_of(half * MB + y * QUART, QUART), QUART)

    def task(kind, what):
        if kind == "columns":
            cols = slice(what * COUNT, (what + 1) * COUNT)
            for dev in range(N_ROW):
                for half in range(2):
                    top = (dev * 2 + half) * QUART
                    cq[top:top + QUART, cols] = column(dev)[quarter(half), cols]
            return
        group, dy = what
        cols = slice(dy * COUNT, (dy + 1) * COUNT)
        if kind == "right":
            for slot in group:
                got = dot(cq[:, cols], r_all[slot, :, cols])
                for half in range(2):
                    for n in range(2 * N_ROW):
                        put(blocks, right_place(slot, half, n), got[n * QUART:(n + 1) * QUART, half * MB:(half + 1) * MB],
                            (kind, group))
        else:
            for n, slot in enumerate(group):
                for half in range(2):
                    top = (n * 2 + half) * QUART
                    rq[top:top + QUART, :] = r_all[slot, quarter(half), cols]
            for dev in range(N_ROW):
                got = dot(rq[...], column(dev)[:, cols])
                for half in range(2):
                    for n in range(8):
                        put(blocks, left_place(dev, half, group[n // 2], n % 2),
                            got[n * QUART:(n + 1) * QUART, half * MB:(half + 1) * MB], (kind, group))
        begun.add((kind, group))

    for kind, what in steps:
        if kind == "wait":
            copies[what].wait_recv()
        elif kind == "start":
            copies[what].start()
        elif kind == "local":
            local()
        elif kind == "distance":
            distance(*what)
        elif kind == "kernel":
            kernel_values(what)
        elif kind == "places":
            places(what)
        else:
            task(kind, what)

    size = out.shape[0] // PIECES
    results = []
    for piece in range(PIECES):
        @pl.loop(0, size)
        def _(m):
            k = piece * size + m
            o_ref[k] = blocks[place_of[k]] * (1.0 / (N_SA * COUNT))

        part = pl.ds(piece * size, size)
        results.append(pltpu.make_async_copy(o_ref.at[part], out.at[part], copy_sems.at[2 + piece]))
        results[-1].start()
    for copy in copies:
        copy.wait_send()
    for copy in results:
        copy.wait()


def normal_tiles(table, pick, states, pool):
    sends, tasks = [], []
    inputs_plan(sends, tasks)
    spread_plan(sends, tasks)
    steps, _ = timetable(sends, tasks)
    whole = N_SA * COUNT
    smem, hbm, anywhere = (pl.BlockSpec(memory_space=space) for space in (pltpu.SMEM, pltpu.HBM, pl.ANY))
    return pl.pallas_call(
        functools.partial(normal_kernel, sends, steps),
        out_shape=jax.ShapeDtypeStruct((table.shape[1], QUART, MB), jnp.float32),
        in_specs=[smem, smem, hbm, hbm],
        out_specs=anywhere,
        scratch_shapes=[
            pltpu.VMEM((N_COL, CENT, whole), jnp.bfloat16),
            pltpu.VMEM((N_ROW - 1, CENT, whole), jnp.bfloat16),
            pltpu.VMEM((2 * 2 * N_ROW * 2 * N_COL, QUART, MB), jnp.float32),
            pltpu.VMEM((CENT, whole), jnp.bfloat16),
            pltpu.VMEM((CENT, COUNT), jnp.bfloat16),
            pltpu.VMEM((N_SA, COUNT, FEAT), jnp.float32),
            pltpu.VMEM((N_SA, CENT, FEAT), jnp.float32),
            pltpu.VMEM((4, share_of(0) // 2, FEAT), jnp.float32),
            pltpu.VMEM(pool.shape, jnp.float32),
            pltpu.VMEM((CENT, COUNT), jnp.float32),
            pltpu.VMEM((CENT, 1), jnp.float32),
            pltpu.SMEM((table.shape[1],), jnp.int32),
            pltpu.VMEM((table.shape[1], QUART, MB), jnp.float32),
            pltpu.SemaphoreType.DMA((2 + PIECES,)),
            pltpu.SemaphoreType.DMA((len(sends),)),
            pltpu.SemaphoreType.DMA((len(sends),)),
        ],
        compiler_params=pltpu.CompilerParams(
            collective_id=0, has_side_effects=True, vmem_limit_bytes=46 * 2**20
        ),
    )(table, pick, states, pool)


def shards(states, pool, pick, tile_table):
    return normal_tiles(tile_table.T, pick, states, pool)


def solution(mesh):
    placed = (P(None, "sa"), P(("row", "col"), "sa"), P(("row", "col")), P(("row", "col"), None))
    return jax.shard_map(
        shards, mesh=mesh, in_specs=placed, out_specs=P(("row", "col"), "sa", None), check_vma=False
    )
```

time: 99.1 us -> 103 us (1.039)
  local copies, waits for them, and re-layouts: 3.09 us -> 5.47 us
  Pallas kernels: 95.9 us -> 97.3 us
    unnamed x1 -> x9, local copies, waits for them, and re-layouts: 3.09 us -> 5.47 us
    pallas_call x1, Pallas kernels: 95.9 us -> 97.3 us  [normal_tiles(): pl.pallas_call(functools.partial(normal_kernel, sends, steps), out_shape=...]
where the time goes in v5:
time: 103 us
  Pallas kernels  97.3 us (94%)
  local copies, waits for them, and re-layouts  5.47 us (5%)
    pallas_call x1, Pallas kernels, normal_tiles(): pl.pallas_call(functools.partial(normal_kernel, sends, steps), out_shape=...  97.3 us
    unnamed x9, local copies, waits for them, and re-layouts  5.47 us

profile of v5, /device:TPU:1, one launch (start us, length us, event | category | flops | bytes accessed | tf_op | source)
XLA Modules:
  0.0 102.8 jit_solution(14783236901939943092)
XLA Ops:
  0.0 0.0 copy-start
  0.0 1.7 %copy-done = f32[2560,256]{1,0:T(8,128)S(1)} copy-done((f32[2560,256]{1,0:T(8,128)S(1)}, f32[2560,256]{1,0:T(8,128)}, u32[]{:S(2)}) %copy-start) | copy-done | bytes 2621464
  1.7 0.0 copy-start.1
  1.7 1.0 %copy-done.1 = f32[512,256]{1,0:T(8,128)S(1)} copy-done((f32[512,256]{1,0:T(8,128)S(1)}, f32[512,256]{1,0:T(8,128)}, u32[]{:S(2)}) %copy-start.1) | copy-done | bytes 524312
  2.8 0.0 copy-start.2
  2.8 0.7 copy-done.2
  3.5 0.0 copy-start.3
  3.5 0.7 copy-done.3
  4.1 97.3 %shard_map.46 = f32[129,32,128]{2,1,0:T(8,128)S(1)} custom-call(s32[2,129]{1,0:T(2,128)S(1)} %bitcast.1, s32[256]{0:T(256)S(1)} %copy-done.3, f32[2560,256]{1,0:T(8,128)S(1)} %copy-done, f32[512,256]{1,0:T(8,128)S(1)} %copy-done.1), custom_call_target="tpu_custom_call" | custom-call | tf_op jit(solution)/shard_map/pallas_call | solution.py:396
  101.5 1.3 %copy.6 = f32[129,32,128]{2,1,0:T(8,128)} copy(f32[129,32,128]{2,1,0:T(8,128)S(1)} %shard_map.46) | data formatting | bytes 4227072
Async XLA Ops:
  0.0 1.7 %copy-start = (f32[2560,256]{1,0:T(8,128)S(1)}, f32[2560,256]{1,0:T(8,128)}, u32[]{:S(2)}) copy-start(f32[2560,256]{1,0:T(8,128)} %states.1) | copy-start | bytes 7864324
  1.7 1.0 %copy-start.1 = (f32[512,256]{1,0:T(8,128)S(1)}, f32[512,256]{1,0:T(8,128)}, u32[]{:S(2)}) copy-start(f32[512,256]{1,0:T(8,128)} %pool.1) | copy-start | bytes 1572868
  2.8 0.7 copy-start.2
  3.5 0.7 copy-start.3

commit v6 on v5

--- a/solution.py
+++ b/solution.py
@@ -31,6 +31,7 @@
 RATE = {"s": 300e3}
 LINK_RATE = 45e3
 LATENCY = 1.7
+LEAF = 3.0
 
 
 class Send:
@@ -69,15 +70,14 @@
     relays = []
     for w in range(2):
         half = share_of(w) // 2
-        need = ("local", *relays) if w else ()
-        relays.append(add("y+", ("H", 2, w, 0, half), ("B", 2 * w, half), half * row_bytes, need, 4 * w))
-        relays.append(add("y-", ("H", 2, w, half, half), ("B", 2 * w + 1, half), half * row_bytes, need, 4 * w))
-    states, late = {}, ((), ("local", *relays[:2]))
+        relays.append(add("y+", ("H", 2, w, 0, half), ("B", 2 * w, half), half * row_bytes, (), 0))
+        relays.append(add("y-", ("H", 2, w, half, half), ("B", 2 * w + 1, half), half * row_bytes, (), 0))
+    states = {}
     for w in range(2):
         share = share_of(w)
         half = share // 2
-        come = {3: [add("y+", ("H", 1, w, 0, share), ("S", 3, 0, w, 0, share), share * row_bytes, late[w], 1 + 4 * w)],
-                1: [add("y-", ("H", 3, w, 0, share), ("S", 1, 0, w, 0, share), share * row_bytes, late[w], 1 + 4 * w)]}
+        come = {3: [add("y+", ("H", 1, w, 0, share), ("S", 3, 0, w, 0, share), share * row_bytes, (), 1 + w)],
+                1: [add("y-", ("H", 3, w, 0, share), ("S", 1, 0, w, 0, share), share * row_bytes, (), 1 + w)]}
         come[2] = [add("y+", ("B", 2 * w, half), ("S", 2, 0, w, 0, half), half * row_bytes, [relays[2 * w]], 0),
                    add("y-", ("B", 2 * w + 1, half), ("S", 2, 0, w, half, half), half * row_bytes, [relays[2 * w + 1]], 0)]
 
@@ -98,7 +98,7 @@
 
     halves = ((0, CENT // 2), (CENT // 2, CENT // 2))
     centres = ring(sends, "y", N_SA, lambda d, part: ("F", d, *cent(part)), lambda part: ("F", 0, *cent(part)), halves,
-                   CENT * row_bytes, ("local", *relays[:2]), 3)
+                   CENT * row_bytes, ("local", *relays), 3)
     tasks.append(("local", None, (), 1.5, True))
     for w in range(2):
         tasks.append(("distance", (0, w), ("local",), 0.5, False))
@@ -106,7 +106,8 @@
         tasks.append(("places", n, ("local",), 0.8, False))
     for w in range(2):
         for d in (3, 1, 2):
-            tasks.append(("distance", (d, w), tuple(states[d, w] + centres[d]), 0.5, True))
+            need = (*states[d, w], *centres[d], *([("kernel", 0)] if w else []))
+            tasks.append(("distance", (d, w), need, 0.5, True))
         tasks.append(("kernel", w, tuple(("distance", (d, w)) for d in range(N_SA)), 0.3, True))
 
 
@@ -146,9 +147,13 @@
         sends.append(Send("s", ("R", dy, 0, 0, cut(EVERY, None)), ("R", dy, 0, 1, cut(EVERY, None)), area(EVERY), need, 30))
         in_r[dy, 1] = [len(sends) - 1]
     for (dy, dz, cols), need in arrived.items():
-        sends.append(Send("s", ("R", dy, dz, 0, cut(cols, None)), ("R", dy, dz, 1, cut(cols, None)), area(cols), need, 30))
+        halved = dz == N_Z // 2 if dy == 0 or cols == Y_FIRST else dy == N_SA // 2
+        for k in need if halved else [None]:
+            part = cut(cols, None) if k is None else sends[k].dst[-1]
+            size = area(cols) if k is None else sends[k].size
+            sends.append(Send("s", ("R", dy, dz, 0, part), ("R", dy, dz, 1, part), size, need if k is None else [k], 30))
+            in_r.setdefault((dy, dz * 2 + 1), []).append(len(sends) - 1)
         in_r.setdefault((dy, dz * 2), []).extend(need)
-        in_r.setdefault((dy, dz * 2 + 1), []).append(len(sends) - 1)
 
     for dy in range(N_SA):
         tasks.append(("columns", dy, tuple(in_c[dy]), 0.15, False))
@@ -162,6 +167,7 @@
 def timetable(sends, tasks):
     free, pending, done, queue, steps = {}, set(range(len(sends))), set(), [], []
     undone = list(range(len(tasks)))
+    relayed = {d for send in sends for d in send.deps} | {d for t in tasks if t[4] for d in t[2]}
 
     def start_ready(now):
         ready = sorted((k for k in pending if all(d in done for d in sends[k].deps)), key=lambda k: (sends[k].rank, k))
@@ -169,7 +175,7 @@
             pending.discard(k)
             link = sends[k].link
             free[link] = max(now, free.get(link, 0.0)) + sends[k].size / RATE.get(link, LINK_RATE)
-            heapq.heappush(queue, (free[link] + LATENCY, k))
+            heapq.heappush(queue, (free[link] + LATENCY + (0.0 if k in relayed else LEAF), k))
             steps.append(("start", k))
 
     core = 0.0
@@ -392,11 +398,11 @@
     spread_plan(sends, tasks)
     steps, _ = timetable(sends, tasks)
     whole = N_SA * COUNT
-    smem, hbm, anywhere = (pl.BlockSpec(memory_space=space) for space in (pltpu.SMEM, pltpu.HBM, pl.ANY))
+    smem, anywhere = pl.BlockSpec(memory_space=pltpu.SMEM), pl.BlockSpec(memory_space=pl.ANY)
     return pl.pallas_call(
         functools.partial(normal_kernel, sends, steps),
         out_shape=jax.ShapeDtypeStruct((table.shape[1], QUART, MB), jnp.float32),
-        in_specs=[smem, smem, hbm, hbm],
+        in_specs=[smem, smem, anywhere, anywhere],
         out_specs=anywhere,
         scratch_shapes=[
             pltpu.VMEM((N_COL, CENT, whole), jnp.bfloat16),
@@ -417,7 +423,7 @@
             pltpu.SemaphoreType.DMA((len(sends),)),
         ],
         compiler_params=pltpu.CompilerParams(
-            collective_id=0, has_side_effects=True, vmem_limit_bytes=46 * 2**20
+            collective_id=0, has_side_effects=True, vmem_limit_bytes=56 * 2**20
         ),
     )(table, pick, states, pool)
 

time: 103 us -> 98.3 us (0.954)
  local copies, waits for them, and re-layouts: 5.47 us -> 3.09 us
  Pallas kernels: 97.3 us -> 95.1 us
    unnamed x9 -> x1, local copies, waits for them, and re-layouts: 5.47 us -> 3.09 us
    pallas_call x1, Pallas kernels: 97.3 us -> 95.1 us  [normal_tiles(): pl.pallas_call(functools.partial(normal_kernel, sends, steps), out_shape=...]
where the time goes in v6:
time: 98.3 us; the launch traced here: 98.2 us
  Pallas kernels  95.1 us (97%)
  local copies, waits for them, and re-layouts  3.09 us (3%)
    pallas_call x1, Pallas kernels, normal_tiles(): pl.pallas_call(functools.partial(normal_kernel, sends, steps), out_shape=...  95.1 us
    unnamed x1, local copies, waits for them, and re-layouts  3.09 us

profile of v6, /device:TPU:1, one launch (start us, length us, event | category | flops | bytes accessed | tf_op | source)
XLA Modules:
  0.0 98.2 jit_solution(3317922726701927274)
XLA Ops:
  0.0 95.1 %shard_map.46 = f32[129,32,128]{2,1,0:T(8,128)} custom-call(s32[2,129]{1,0:T(2,128)} %bitcast.1, s32[256]{0:T(256)} %pick.1, f32[2560,256]{1,0:T(8,128)} %states.1, f32[512,256]{1,0:T(8,128)} %pool.1), custom_call_target="tpu_custom_call" | custom-call | tf_op jit(solution)/shard_map/pallas_call | solution.py:402
  95.1 3.1 %copy.6 = f32[129,32,128]{2,1,0:T(8,128)} copy(f32[129,32,128]{2,1,0:T(8,128)} %shard_map.46) | data formatting | bytes 4227072

commit v7 on v4

--- a/solution.py
+++ b/solution.py
@@ -30,6 +30,7 @@
 RATE = {"s": 300e3}
 LINK_RATE = 45e3
 LATENCY = 1.7
+LEAF = 3.0
 
 
 class Send:
@@ -149,6 +150,7 @@
 def timetable(sends, tasks, local):
     free, pending, done, queue, steps = {}, set(range(len(sends))), set(), [], []
     undone = list(range(len(tasks)))
+    relayed = {d for send in sends for d in send.deps}
 
     def start_ready(now):
         ready = sorted((k for k in pending if all(d in done for d in sends[k].deps)), key=lambda k: (sends[k].rank, k))
@@ -156,7 +158,7 @@
             pending.discard(k)
             link = sends[k].link
             free[link] = max(now, free.get(link, 0.0)) + sends[k].size / RATE.get(link, LINK_RATE)
-            heapq.heappush(queue, (free[link] + LATENCY, k))
+            heapq.heappush(queue, (free[link] + LATENCY + (0.0 if k in relayed or local is not None else LEAF), k))
             steps.append(("start", k))
 
     core = 0.0
@@ -253,7 +255,9 @@
     def distance(d):
         sample, centre = s_all[d], f_all[d]
         cross = dot(centre, sample, lax.Precision.HIGHEST)
-        norms = dot(jnp.ones((8, FEAT), jnp.float32), sample * sample, lax.Precision.HIGHEST)
+        squares = sample * sample
+        squares = squares[:, :MB] + squares[:, MB:]
+        norms = jnp.sum(squares.T, axis=0, keepdims=True)
         own = jnp.sum(centre * centre, axis=1, keepdims=True)
         if d:
             inner[...] += cross
@@ -332,7 +336,7 @@
 
     first = copies_of(plans[0], first_out, first_in)
     run(first, steps[0])
-    total = sample_norms[:1, :] + centre_norms[...] - 2.0 * inner[...]
+    total = sample_norms[...] + centre_norms[...] - 2.0 * inner[...]
     r_all[0, :, :COUNT] = jnp.exp((2.0 * F - total) / (4.0 * math.sqrt(F))).astype(jnp.bfloat16)
     second = copies_of(plans[1], out_sems, in_sems)
     for kind, what in steps[1]:
@@ -392,7 +396,7 @@
             pltpu.VMEM((2, SHARE // 2, FEAT), jnp.float32),
             pltpu.VMEM(pool.shape, jnp.float32),
             pltpu.VMEM((CENT, COUNT), jnp.float32),
-            pltpu.VMEM((8, COUNT), jnp.float32),
+            pltpu.VMEM((1, COUNT), jnp.float32),
             pltpu.VMEM((CENT, 1), jnp.float32),
             pltpu.SMEM((table.shape[1],), jnp.int32),
             pltpu.SemaphoreType.DMA((2,)),

time: 99.1 us -> 101 us (1.019)
  Pallas kernels: 95.9 us -> 97.5 us
    pallas_call x1, Pallas kernels: 95.9 us -> 97.5 us  [normal_tiles(): pl.pallas_call(functools.partial(normal_kernel, [first, second], steps),...]
where the time goes in v7:
time: 101 us
  Pallas kernels  97.5 us (97%)
  local copies, waits for them, and re-layouts  3.09 us (3%)
    pallas_call x1, Pallas kernels, normal_tiles(): pl.pallas_call(functools.partial(normal_kernel, [first, second], steps),...  97.5 us
    unnamed x1, local copies, waits for them, and re-layouts  3.09 us

profile of v7, /device:TPU:1, one launch (start us, length us, event | category | flops | bytes accessed | tf_op | source)
XLA Modules:
  0.0 100.6 jit_solution(9580082679322143435)
XLA Ops:
  0.0 97.5 %shard_map.46 = f32[129,32,128]{2,1,0:T(8,128)} custom-call(s32[2,129]{1,0:T(2,128)} %bitcast.1, s32[256]{0:T(256)} %pick.1, f32[2560,256]{1,0:T(8,128)} %states.1, f32[512,256]{1,0:T(8,128)} %pool.1), custom_call_target="tpu_custom_call" | custom-call | tf_op jit(solution)/shard_map/pallas_call | solution.py:383
  97.5 3.1 %copy.6 = f32[129,32,128]{2,1,0:T(8,128)} copy(f32[129,32,128]{2,1,0:T(8,128)} %shard_map.46) | data formatting | bytes 4227072

commit v8 on v6

--- a/solution.py
+++ b/solution.py
@@ -184,7 +184,7 @@
         coming = queue[0][0] if queue else math.inf
         ready = [t for t in undone if all(d in done for d in tasks[t][2])]
         ready.sort(key=lambda t: not tasks[t][4])
-        if ready and coming - core >= (0.0 if tasks[ready[0]][4] else 0.6 * tasks[ready[0]][3]):
+        if ready and coming - core >= (0.0 if tasks[ready[0]][4] else 0.3 * tasks[ready[0]][3]):
             kind, what, _, span, _ = tasks[ready[0]]
             undone.remove(ready[0])
             core += span

time: 98.3 us -> 97.9 us (level)
  no operation moved by 1% of the time
where the time goes in v8:
time: 97.9 us; the launch traced here: 97.7 us
  Pallas kernels  94.6 us (97%)
  local copies, waits for them, and re-layouts  3.09 us (3%)
    pallas_call x1, Pallas kernels, normal_tiles(): pl.pallas_call(functools.partial(normal_kernel, sends, steps), out_shape=...  94.6 us
    unnamed x1, local copies, waits for them, and re-layouts  3.09 us

profile of v8, /device:TPU:1, one launch (start us, length us, event | category | flops | bytes accessed | tf_op | source)
XLA Modules:
  0.0 97.7 jit_solution(8056326654301436791)
XLA Ops:
  0.0 94.6 %shard_map.46 = f32[129,32,128]{2,1,0:T(8,128)} custom-call(s32[2,129]{1,0:T(2,128)} %bitcast.1, s32[256]{0:T(256)} %pick.1, f32[2560,256]{1,0:T(8,128)} %states.1, f32[512,256]{1,0:T(8,128)} %pool.1), custom_call_target="tpu_custom_call" | custom-call | tf_op jit(solution)/shard_map/pallas_call | solution.py:402
  94.6 3.1 %copy.6 = f32[129,32,128]{2,1,0:T(8,128)} copy(f32[129,32,128]{2,1,0:T(8,128)} %shard_map.46) | data formatting | bytes 4227072
